TPU v7x, 256 devices: a whole 4x4x8 slice. The times are simulated.
256 devices in a mesh: ctx: 16 (over z, x_lo), head: 16 (over x_hi, y, core).
Axes of the slice: x: 4 (x_hi: 2, x_lo: 2; x = x_hi * 2 + x_lo), y: 4, z: 8, core: 2. Of those that a mesh axis runs over, the one named last changes fastest.
Arguments:
- queries: bfloat16 [32768, 64, 128], P(('ctx', 'head')), may hold values from -100 to 100
- keys: bfloat16 [32768, 8, 128], P(('ctx', 'head')), may hold values from -6 to 6
- values: bfloat16 [32768, 8, 128], P(('ctx', 'head')), may hold values from -6 to 6
- outputs: bfloat16 [32768, 64, 128], P(('ctx', 'head')), may hold values from -6 to 6
- out_grad: bfloat16 [32768, 64, 128], P(('ctx', 'head')), may hold values from -6 to 6
- segments: int32 [32768], replicated, may hold values from 0 to 255, never falling along the last dimension, each value on 1 to 512 neighbouring positions
Outputs:
- query_grad: bfloat16 [32768, 64, 128], P(('ctx', 'head'))
- key_grad: bfloat16 [32768, 8, 128], P(('ctx', 'head'))
- value_grad: bfloat16 [32768, 8, 128], P(('ctx', 'head'))
Inputs may be any that keep to these rules, and one draw needn't show every extreme that they name: `segments`: the document number never falls along the pack; every document has 1 to 512 tokens and one has exactly 512.
All inputs are finite; a program needn't handle non-finite values.
Results may differ from a plain program's by a relative error of at most 0.007.
Values may be sent and summed in bfloat16 or wider, within the bound.
No kernel may reach another device: no remote copies, remote signals or barrier semaphores. Data moves between devices by JAX's collectives and lax.ppermute only.
A program may use at most 128 MiB of HBM per device.

v0:
```python
import jax
import jax.numpy as jnp
from jax import lax
from jax.sharding import PartitionSpec as P


def shifted(block, axis, distance):
    devices = range(lax.axis_size(axis))
    route = [(i - distance, i) for i in devices if i - distance in devices]
    return lax.ppermute(block, axis, route)


def heads_layout(queries, keys, values, outputs, out_grad, segments):
    head_count = lax.axis_size("head")
    kv_heads = keys.shape[1]
    repeats = max(1, head_count // kv_heads)
    keys_wide = jnp.repeat(keys, repeats, axis=1)
    values_wide = jnp.repeat(values, repeats, axis=1)
    q_local, k_local, v_local, o_local, g_local = (
        lax.all_to_all(queries, "head", split_axis=1, concat_axis=0, tiled=True),
        lax.all_to_all(keys_wide, "head", split_axis=1, concat_axis=0, tiled=True),
        lax.all_to_all(values_wide, "head", split_axis=1, concat_axis=0, tiled=True),
        lax.all_to_all(outputs, "head", split_axis=1, concat_axis=0, tiled=True),
        lax.all_to_all(out_grad, "head", split_axis=1, concat_axis=0, tiled=True),
    )
    seq_rows = q_local.shape[0]
    span = seq_rows // 4
    block = min(512, seq_rows)
    window = span + block
    kv_local = k_local.shape[1]
    group = q_local.shape[1] // kv_local
    head_dim = q_local.shape[2]
    scale = head_dim ** (-0.5)
    prev_keys, prev_values = shifted((k_local, v_local), "ctx", 1)
    prev_keys = prev_keys[seq_rows - span :]
    prev_values = prev_values[seq_rows - span :]
    keys_ext = jnp.concatenate([prev_keys, k_local], axis=0)
    values_ext = jnp.concatenate([prev_values, v_local], axis=0)
    shard_start = lax.axis_index("ctx") * seq_rows
    seg_pad = jnp.concatenate([jnp.full((span,), -1, jnp.int32), segments], axis=0)
    seg_keys = lax.dynamic_slice_in_dim(seg_pad, shard_start, seq_rows + span, 0)
    seg_query = lax.dynamic_slice_in_dim(segments, shard_start, seq_rows, 0)
    col_index = jnp.arange(window, dtype=jnp.int32)
    row_index = jnp.arange(block, dtype=jnp.int32)
    causal = col_index[None, :] <= row_index[:, None] + span
    block_starts = list(range(0, seq_rows, block))

    def scores(begin):
        q_block = q_local[begin : begin + block].reshape(block, kv_local, group, head_dim)
        k_window = keys_ext[begin : begin + window]
        same_doc = (
            seg_query[begin : begin + block][:, None] == seg_keys[begin : begin + window][None, :]
        )
        raw = scale * jnp.einsum(
            "bkgd,wkd->kgbw", q_block, k_window, preferred_element_type=jnp.float32
        )
        return (jnp.where(same_doc & causal, raw, -jnp.inf), q_block, k_window)

    log_sums = []
    for begin in block_starts:
        masked, q_block, k_window = scores(begin)
        top = jnp.max(masked, axis=-1)
        log_sums.append(top + jnp.log(jnp.sum(jnp.exp(masked - top[..., None]), axis=-1)))
    delta_all = jnp.sum(o_local.astype(jnp.float32) * g_local.astype(jnp.float32), axis=-1)
    grad_keys = jnp.zeros((span + seq_rows, kv_local, head_dim), jnp.float32)
    grad_values = jnp.zeros((span + seq_rows, kv_local, head_dim), jnp.float32)
    query_parts = []
    for number, begin in enumerate(block_starts):
        masked, q_block, k_window = scores(begin)
        v_window = values_ext[begin : begin + window]
        prob = jnp.exp(masked - log_sums[number][..., None])
        prob_low = prob.astype(jnp.bfloat16)
        g_block = g_local[begin : begin + block].reshape(block, kv_local, group, head_dim)
        d_block = jnp.transpose(
            delta_all[begin : begin + block].reshape(block, kv_local, group), (1, 2, 0)
        )
        d_prob = jnp.einsum("bkgd,wkd->kgbw", g_block, v_window, preferred_element_type=jnp.float32)
        d_score = (prob * (d_prob - d_block[..., None])).astype(jnp.bfloat16)
        query_part = scale * jnp.einsum(
            "kgbw,wkd->bkgd", d_score, k_window, preferred_element_type=jnp.float32
        )
        query_parts.append(
            query_part.astype(jnp.bfloat16).reshape(block, kv_local * group, head_dim)
        )
        key_part = scale * jnp.einsum(
            "kgbw,bkgd->wkd", d_score, q_block, preferred_element_type=jnp.float32
        )
        value_part = jnp.einsum(
            "kgbw,bkgd->wkd", prob_low, g_block, preferred_element_type=jnp.float32
        )
        grad_keys = grad_keys.at[begin : begin + window].add(key_part)
        grad_values = grad_values.at[begin : begin + window].add(value_part)
    query_local = jnp.concatenate(query_parts, axis=0)
    padding = jnp.zeros((seq_rows - span, kv_local, head_dim), jnp.float32)
    lead_keys = jnp.concatenate([padding, grad_keys[:span]], axis=0)
    lead_values = jnp.concatenate([padding, grad_values[:span]], axis=0)
    back_keys, back_values = (
        shifted(lead_keys.astype(jnp.bfloat16), "ctx", -1).astype(lead_keys.dtype),
        shifted(lead_values.astype(jnp.bfloat16), "ctx", -1).astype(lead_values.dtype),
    )
    own_keys = grad_keys[span:] + back_keys
    own_values = grad_values[span:] + back_values
    query_home = lax.all_to_all(query_local, "head", split_axis=0, concat_axis=1, tiled=True)
    keys_home, values_home = (
        lax.all_to_all(own_keys, "head", split_axis=0, concat_axis=1, tiled=True),
        lax.all_to_all(own_values, "head", split_axis=0, concat_axis=1, tiled=True),
    )
    token_rows = keys_home.shape[0]
    key_grad = jnp.sum(keys_home.reshape(token_rows, kv_heads, repeats, head_dim), axis=2).astype(
        jnp.bfloat16
    )
    value_grad = jnp.sum(
        values_home.reshape(token_rows, kv_heads, repeats, head_dim), axis=2
    ).astype(jnp.bfloat16)
    return (query_home, key_grad, value_grad)


def shards(queries, keys, values, outputs, out_grad, segments):
    return heads_layout(queries, keys, values, outputs, out_grad, segments)


def solution(mesh):
    return jax.shard_map(
        shards,
        mesh=mesh,
        in_specs=(
            P(("ctx", "head"), None, None),
            P(("ctx", "head"), None, None),
            P(("ctx", "head"), None, None),
            P(("ctx", "head"), None, None),
            P(("ctx", "head"), None, None),
            P(),
        ),
        out_specs=(
            P(("ctx", "head"), None, None),
            P(("ctx", "head"), None, None),
            P(("ctx", "head"), None, None),
        ),
        check_vma=False,
    )
```

profile of v0, /device:TPU:121, one launch (start us, length us, event | category | flops | bytes accessed | tf_op | source)
XLA Modules:
  0.0 331.4 jit_solution(9475756991510683676)
XLA Ops:
  2.5 7.5 %all-to-all-start = ((bf16[128,16,128]{2,0,1:T(8,128)(2,1)}), bf16[128,16,128]{2,0,1:T(8,128)(2,1)S(1)}, u32[]{:S(2)}, u32[]{:S(2)}) async-start(bf16[128,16,128]{2,0,1:T(8,128)(2,1)} %bitcast), calls=%async_computation | async-start | bytes 1048576 | tf_op jit(solution)/shard_map/all_to_all | solution.py:21
  11.0 9.4 %all-to-all-done = bf16[128,16,128]{2,0,1:T(8,128)(2,1)S(1)} async-done(((bf16[128,16,128]{2,0,1:T(8,128)(2,1)}), bf16[128,16,128]{2,0,1:T(8,128)(2,1)S(1)}, u32[]{:S(2)}, u32[]{:S(2)}) %all-to-all-start) | async-done | bytes 524320 | tf_op jit(solution)/shard_map/all_to_all | solution.py:21
  21.3 6.1 %all-to-all-start.2 = ((bf16[128,16,128]{2,0,1:T(8,128)(2,1)}), bf16[128,16,128]{2,0,1:T(8,128)(2,1)}, u32[]{:S(2)}, u32[]{:S(2)}) async-start(bf16[128,16,128]{2,0,1:T(8,128)(2,1)} %bitcast.12), calls=%async_computation.2 | async-start | bytes 1048576 | tf_op jit(solution)/shard_map/all_to_all | solution.py:22
  27.4 4.3 %copy.24 = bf16[128,64,128]{2,0,1:T(8,128)(2,1)} copy(bf16[128,64,128]{2,1,0:T(8,128)(2,1)} %param.22) | data formatting | bytes 4194304 | tf_op args[0]
  31.6 6.2 %all-to-all-done.2 = bf16[128,16,128]{2,0,1:T(8,128)(2,1)} async-done(((bf16[128,16,128]{2,0,1:T(8,128)(2,1)}), bf16[128,16,128]{2,0,1:T(8,128)(2,1)}, u32[]{:S(2)}, u32[]{:S(2)}) %all-to-all-start.2) | async-done | bytes 524320 | tf_op jit(solution)/shard_map/all_to_all | solution.py:22
  37.9 5.7 %all-to-all-start.1 = ((bf16[128,64,128]{2,0,1:T(8,128)(2,1)}), bf16[128,64,128]{2,0,1:T(8,128)(2,1)S(1)}, u32[]{:S(2)}, u32[]{:S(2)}) async-start(bf16[128,64,128]{2,0,1:T(8,128)(2,1)} %copy.24), calls=%async_computation.1 | async-start | bytes 4194304 | tf_op jit(solution)/shard_map/all_to_all | solution.py:20
  43.5 4.3 %copy.29 = bf16[128,64,128]{2,0,1:T(8,128)(2,1)} copy(bf16[128,64,128]{2,1,0:T(8,128)(2,1)} %param.25) | data formatting | bytes 4194304 | tf_op args[3]
  47.9 25.2 %all-to-all-done.1 = bf16[128,64,128]{2,0,1:T(8,128)(2,1)S(1)} async-done(((bf16[128,64,128]{2,0,1:T(8,128)(2,1)}), bf16[128,64,128]{2,0,1:T(8,128)(2,1)S(1)}, u32[]{:S(2)}, u32[]{:S(2)}) %all-to-all-start.1) | async-done | bytes 2097184 | tf_op jit(solution)/shard_map/all_to_all | solution.py:20
  74.4 5.9 %all-to-all-start.4 = ((bf16[128,64,128]{2,0,1:T(8,128)(2,1)}), bf16[128,64,128]{2,0,1:T(8,128)(2,1)S(1)}, u32[]{:S(2)}, u32[]{:S(2)}) async-start(bf16[128,64,128]{2,0,1:T(8,128)(2,1)} %copy.29), calls=%async_computation.4 | async-start | bytes 4194304 | tf_op jit(solution)/shard_map/all_to_all | solution.py:23
  80.3 4.3 %copy.27 = bf16[128,64,128]{2,0,1:T(8,128)(2,1)} copy(bf16[128,64,128]{2,1,0:T(8,128)(2,1)} %param.26) | data formatting | bytes 4194304 | tf_op args[4]
  84.6 25.2 %all-to-all-done.4 = bf16[128,64,128]{2,0,1:T(8,128)(2,1)S(1)} async-done(((bf16[128,64,128]{2,0,1:T(8,128)(2,1)}), bf16[128,64,128]{2,0,1:T(8,128)(2,1)S(1)}, u32[]{:S(2)}, u32[]{:S(2)}) %all-to-all-start.4) | async-done | bytes 2097184 | tf_op jit(solution)/shard_map/all_to_all | solution.py:23
  111.2 6.1 %all-to-all-start.3 = ((bf16[128,64,128]{2,0,1:T(8,128)(2,1)}), bf16[128,64,128]{2,0,1:T(8,128)(2,1)S(1)}, u32[]{:S(2)}, u32[]{:S(2)}) async-start(bf16[128,64,128]{2,0,1:T(8,128)(2,1)} %copy.27), calls=%async_computation.3 | async-start | bytes 4194304 | tf_op jit(solution)/shard_map/all_to_all | solution.py:24
  120.0 5.9 %collective-permute-start = (bf16[2048,1,128]{2,0,1:T(8,128)(2,1)S(1)}, bf16[2048,1,128]{2,0,1:T(8,128)(2,1)S(1)}, u32[]{:S(2)}, u32[]{:S(2)}) collective-permute-start(bf16[2048,1,128]{2,0,1:T(8,128)(2,1)S(1)} %bitcast.453), channel_id=1, source_target_pairs={{0,16},{16,32},{32,48},{48,64},{64,80},{80,96},{96,112},{112,128},... | collective-permute-start | bytes 1572872 | tf_op jit(solution)/shard_map/ppermute | solution.py:10
  131.8 20.2 %collective-permute-done.1 = bf16[2048,1,128]{2,0,1:T(8,128)(2,1)S(1)} collective-permute-done((bf16[2048,1,128]{2,0,1:T(8,128)(2,1)}, bf16[2048,1,128]{2,0,1:T(8,128)(2,1)S(1)}, u32[]{:S(2)}, u32[]{:S(2)}) %collective-permute-start.1) | collective-permute-done | bytes 524320 | tf_op jit(solution)/shard_map/ppermute | solution.py:10
  152.7 10.5 %collective-permute-done = bf16[2048,1,128]{2,0,1:T(8,128)(2,1)S(1)} collective-permute-done((bf16[2048,1,128]{2,0,1:T(8,128)(2,1)S(1)}, bf16[2048,1,128]{2,0,1:T(8,128)(2,1)S(1)}, u32[]{:S(2)}, u32[]{:S(2)}) %collective-permute-start) | collective-permute-done | bytes 524320 | tf_op jit(solution)/shard_map/ppermute | solution.py:10
  168.7 3.3 %fusion.24 = f32[16,128,4]{1,0,2:T(8,128)S(1)} fusion(f32[128,16,4,128]{3,0,2,1:T(8,128)} %bitcast_convert_fusion, bf16[128,16,4,128]{3,0,2,1:T(8,128)(2,1)S(1)} %bitcast.452), kind=kLoop, calls=%fused_computation.41 | loop fusion | flops 3137536 | bytes 6324224 | tf_op jit(solution)/shard_map/reduce_sum | solution.py:64
  182.8 3.9 %fusion.20 = bf16[4,512,1024]{1,2,0:T(8,128)(2,1)S(1)} fusion(f32[1024,512,4]{1,0,2:T(8,128)S(1)} %get-tuple-element.139, f32[4,512]{1,0:T(4,128)S(1)} %bitcast.492, f32[4,512]{1,0:T(4,128)S(1)} %log_add_fusion.3, pred[512,1024]{0,1:T(8,128)(4,1)S(1)} %copy-done.9, bf16[512,4,128]{2,0,1:T(8,128)(2,1)S(1)} %bitcast.485, bf16[2048,1,128]{2,0,1:T(8,128)(2,1)} %bitcast.15, ...), kind=kOutput, calls=%fused_computation.36 | convolution fusion | flops 549978112 | bytes 14303232 | tf_op jit(solution)/shard_map/bkgd,wkd->kgbw/dot_general | solution.py:77
  192.7 3.8 %exponential_reduce_fusion = (f32[4,512]{1,0:T(4,128)S(1)}, f32[4,512]{1,0:T(4,128)S(1)}) fusion(f32[1024,512,4]{1,0,2:T(8,128)S(1)} %get-tuple-element.133, f32[4,512]{1,0:T(4,128)S(1)} %get-tuple-element.132, pred[512,1024]{0,1:T(8,128)(4,1)S(1)} %get-tuple-element.129, f32[4,512]{1,0:T(4,128)S(1)} %get-tuple-element.134, ...), kind=kLoop, calls=%fused_computation.17 | loop fusion | flops 16773120 | bytes 17858560 | tf_op jit(solution)/shard_map/reduce_sum | solution.py:63
  205.1 5.6 %fusion.22 = bf16[4,512,1024]{1,2,0:T(8,128)(2,1)} fusion(f32[1024,512,4]{1,0,2:T(8,128)S(1)} %get-tuple-element.135, f32[4,512]{1,0:T(4,128)S(1)} %bitcast.491, f32[4,512]{1,0:T(4,128)S(1)} %log_add_fusion.1, pred[512,1024]{0,1:T(8,128)(4,1)} %get-tuple-element.130, bf16[1024,128,1]{1,0,2:T(8,128)(2,1)S(1)} %bitcast.488, bf16[512,4,128]{2,0,1:T(8,128)(2,1)} %bitcast.482), kind=kOutput, calls=%fused_computation.38 | convolution fusion | flops 549453824 | bytes 13910016 | tf_op jit(solution)/shard_map/bkgd,wkd->kgbw/dot_general | solution.py:77
  210.7 4.4 %fusion.21 = bf16[4,512,1024]{1,2,0:T(8,128)(2,1)S(1)} fusion(f32[1024,512,4]{1,0,2:T(8,128)S(1)} %get-tuple-element.137, f32[4,512]{1,0:T(4,128)S(1)} %bitcast.490, f32[4,512]{1,0:T(4,128)S(1)} %log_add_fusion.2, pred[512,1024]{0,1:T(8,128)(4,1)S(1)} %copy-done.7, bf16[1024,128,1]{1,0,2:T(8,128)(2,1)S(1)} %bitcast.487, bf16[512,4,128]{2,0,1:T(8,128)(2,1)} %bitcast.480), kind=kOutput, calls=%fused_computation.37 | convolution fusion | flops 549453824 | bytes 13910016 | tf_op jit(solution)/shard_map/bkgd,wkd->kgbw/dot_general | solution.py:77
  220.4 3.0 fusion.23
  224.8 3.6 %collective-permute-start.2 = (bf16[2048,1,128]{2,0,1:T(8,128)(2,1)S(1)}, bf16[2048,1,128]{2,0,1:T(8,128)(2,1)S(1)}, u32[]{:S(2)}, u32[]{:S(2)}) collective-permute-start(bf16[2048,1,128]{2,0,1:T(8,128)(2,1)S(1)} %concatenate.38), channel_id=1, source_target_pairs={{16,0},{32,16},{48,32},{64,48},{80,64},{96,80},{112,96},{128,112},... | collective-permute-start | bytes 1572872 | tf_op jit(solution)/shard_map/ppermute | solution.py:10
  233.7 6.6 %collective-permute-done.2 = bf16[2048,1,128]{2,0,1:T(8,128)(2,1)S(1)} collective-permute-done((bf16[2048,1,128]{2,0,1:T(8,128)(2,1)S(1)}, bf16[2048,1,128]{2,0,1:T(8,128)(2,1)S(1)}, u32[]{:S(2)}, u32[]{:S(2)}) %collective-permute-start.2) | collective-permute-done | bytes 524320 | tf_op jit(solution)/shard_map/ppermute | solution.py:10
  241.4 9.4 %all-to-all-start.6 = ((f32[2048,1,128]{2,1,0:T(1,128)}), f32[2048,1,128]{2,1,0:T(1,128)S(1)}, u32[]{:S(2)}, u32[]{:S(2)}) async-start(f32[2048,1,128]{2,1,0:T(1,128)} %bitcast.468), calls=%async_computation.6 | async-start | bytes 2097152 | tf_op jit(solution)/shard_map/all_to_all | solution.py:105
  250.8 3.8 %fusion.58 = bf16[512,4,128]{0,2,1:T(8,128)(2,1)} fusion(bf16[4,512,1024]{1,2,0:T(8,128)(2,1)} %fusion.22, bf16[1024,128,1]{1,0,2:T(8,128)(2,1)} %bitcast.476), kind=kOutput, calls=%fused_computation.71 | convolution fusion | flops 537395200 | bytes 4980736 | tf_op jit(solution)/shard_map/kgbw,wkd->bkgd/dot_general | solution.py:79
  256.7 14.3 %all-to-all-done.6 = f32[2048,1,128]{2,1,0:T(1,128)S(1)} async-done(((f32[2048,1,128]{2,1,0:T(1,128)}), f32[2048,1,128]{2,1,0:T(1,128)S(1)}, u32[]{:S(2)}, u32[]{:S(2)}) %all-to-all-start.6) | async-done | bytes 1048608 | tf_op jit(solution)/shard_map/all_to_all | solution.py:105
  271.0 6.3 %all-to-all-start.7 = ((f32[2048,1,128]{2,1,0:T(1,128)}), f32[2048,1,128]{2,1,0:T(1,128)}, u32[]{:S(2)}, u32[]{:S(2)}) async-start(f32[2048,1,128]{2,1,0:T(1,128)} %bitcast.467), calls=%async_computation.7 | async-start | bytes 2097152 | tf_op jit(solution)/shard_map/all_to_all | solution.py:106
  277.3 3.1 fusion.57
  280.5 3.0 fusion.60
  287.1 6.8 %all-to-all-done.7 = f32[2048,1,128]{2,1,0:T(1,128)} async-done(((f32[2048,1,128]{2,1,0:T(1,128)}), f32[2048,1,128]{2,1,0:T(1,128)}, u32[]{:S(2)}, u32[]{:S(2)}) %all-to-all-start.7) | async-done | bytes 1048608 | tf_op jit(solution)/shard_map/all_to_all | solution.py:106
  293.9 5.2 %all-to-all-start.5 = ((bf16[2048,4,128]{2,1,0:T(4,128)(2,1)}), bf16[2048,4,128]{2,1,0:T(4,128)(2,1)S(1)}, u32[]{:S(2)}, u32[]{:S(2)}) async-start(bf16[2048,4,128]{2,1,0:T(4,128)(2,1)} %copy.39), calls=%async_computation.5 | async-start | bytes 4194304 | tf_op jit(solution)/shard_map/all_to_all | solution.py:103
  303.5 25.1 %all-to-all-done.5 = bf16[2048,4,128]{2,1,0:T(4,128)(2,1)S(1)} async-done(((bf16[2048,4,128]{2,1,0:T(4,128)(2,1)}), bf16[2048,4,128]{2,1,0:T(4,128)(2,1)S(1)}, u32[]{:S(2)}, u32[]{:S(2)}) %all-to-all-start.5) | async-done | bytes 2097184 | tf_op jit(solution)/shard_map/all_to_all | solution.py:103
  (124 shorter events, 71.8 us)
Async XLA Ops:
  2.5 17.8 %all-to-all-start = ((bf16[128,16,128]{2,0,1:T(8,128)(2,1)}), bf16[128,16,128]{2,0,1:T(8,128)(2,1)S(1)}, u32[]{:S(2)}, u32[]{:S(2)}) async-start(bf16[128,16,128]{2,0,1:T(8,128)(2,1)} %bitcast), calls=%async_computation | async-start | bytes 1048576 | tf_op jit(solution)/shard_map/all_to_all | solution.py:21
  21.3 16.6 %all-to-all-start.2 = ((bf16[128,16,128]{2,0,1:T(8,128)(2,1)}), bf16[128,16,128]{2,0,1:T(8,128)(2,1)}, u32[]{:S(2)}, u32[]{:S(2)}) async-start(bf16[128,16,128]{2,0,1:T(8,128)(2,1)} %bitcast.12), calls=%async_computation.2 | async-start | bytes 1048576 | tf_op jit(solution)/shard_map/all_to_all | solution.py:22
  37.9 35.2 %all-to-all-start.1 = ((bf16[128,64,128]{2,0,1:T(8,128)(2,1)}), bf16[128,64,128]{2,0,1:T(8,128)(2,1)S(1)}, u32[]{:S(2)}, u32[]{:S(2)}) async-start(bf16[128,64,128]{2,0,1:T(8,128)(2,1)} %copy.24), calls=%async_computation.1 | async-start | bytes 4194304 | tf_op jit(solution)/shard_map/all_to_all | solution.py:20
  43.5 73.8 %copy-start.27 = (s32[32768]{0:T(1024)S(1)}, s32[32768]{0:T(1024)}, u32[]{:S(2)}) copy-start(s32[32768]{0:T(1024)} %param.27) | copy-start | bytes 393220
  74.4 35.4 %all-to-all-start.4 = ((bf16[128,64,128]{2,0,1:T(8,128)(2,1)}), bf16[128,64,128]{2,0,1:T(8,128)(2,1)S(1)}, u32[]{:S(2)}, u32[]{:S(2)}) async-start(bf16[128,64,128]{2,0,1:T(8,128)(2,1)} %copy.29), calls=%async_computation.4 | async-start | bytes 4194304 | tf_op jit(solution)/shard_map/all_to_all | solution.py:23
  111.2 57.6 %all-to-all-start.3 = ((bf16[128,64,128]{2,0,1:T(8,128)(2,1)}), bf16[128,64,128]{2,0,1:T(8,128)(2,1)S(1)}, u32[]{:S(2)}, u32[]{:S(2)}) async-start(bf16[128,64,128]{2,0,1:T(8,128)(2,1)} %copy.27), calls=%async_computation.3 | async-start | bytes 4194304 | tf_op jit(solution)/shard_map/all_to_all | solution.py:24
  117.3 48.9 %copy-start.1 = (bf16[128,64,128]{2,0,1:T(8,128)(2,1)S(1)}, bf16[128,64,128]{2,0,1:T(8,128)(2,1)}, u32[]{:S(2)}) copy-start(bf16[128,64,128]{2,0,1:T(8,128)(2,1)} %copy-done) | copy-start | bytes 6291460
  117.5 34.5 %collective-permute-start.1 = (bf16[2048,1,128]{2,0,1:T(8,128)(2,1)}, bf16[2048,1,128]{2,0,1:T(8,128)(2,1)S(1)}, u32[]{:S(2)}, u32[]{:S(2)}) collective-permute-start(bf16[2048,1,128]{2,0,1:T(8,128)(2,1)} %bitcast.15), channel_id=1, source_target_pairs={{0,16},{16,32},{32,48},{48,64},{64,80},{80,96},{96,112},{112,128},... | collective-permute-start | bytes 1572872 | tf_op jit(solution)/shard_map/ppermute | solution.py:10
  120.0 43.1 %collective-permute-start = (bf16[2048,1,128]{2,0,1:T(8,128)(2,1)S(1)}, bf16[2048,1,128]{2,0,1:T(8,128)(2,1)S(1)}, u32[]{:S(2)}, u32[]{:S(2)}) collective-permute-start(bf16[2048,1,128]{2,0,1:T(8,128)(2,1)S(1)} %bitcast.453), channel_id=1, source_target_pairs={{0,16},{16,32},{32,48},{48,64},{64,80},{80,96},{96,112},{112,128},... | collective-permute-start | bytes 1572872 | tf_op jit(solution)/shard_map/ppermute | solution.py:10
  186.7 4.0 %copy-start.8 = (pred[512,1024]{0,1:T(8,128)(4,1)S(1)}, pred[512,1024]{0,1:T(8,128)(4,1)}, u32[]{:S(2)}) copy-start(pred[512,1024]{0,1:T(8,128)(4,1)} %get-tuple-element.130) | copy-start | bytes 1572868
  186.8 4.0 %copy-start.12 = (bf16[4,128,4,128]{3,1,0,2:T(8,128)(2,1)S(1)}, bf16[4,128,4,128]{3,1,0,2:T(8,128)(2,1)}, u32[]{:S(2)}) copy-start(bf16[4,128,4,128]{3,1,0,2:T(8,128)(2,1)} %get-tuple-element.108) | copy-start | bytes 1572868
  186.8 4.0 %copy-start.19 = (bf16[8,128,1,128]{3,1,0,2:T(8,128)(2,1)S(1)}, bf16[8,128,1,128]{3,1,0,2:T(8,128)(2,1)}, u32[]{:S(2)}) copy-start(bf16[8,128,1,128]{3,1,0,2:T(8,128)(2,1)} %get-tuple-element.114) | copy-start | bytes 786436
  192.7 3.9 %copy-start.7 = (pred[512,1024]{0,1:T(8,128)(4,1)S(1)}, pred[512,1024]{0,1:T(8,128)(4,1)}, u32[]{:S(2)}) copy-start(pred[512,1024]{0,1:T(8,128)(4,1)} %get-tuple-element.131) | copy-start | bytes 1572868
  192.7 3.9 %copy-start.13 = (bf16[4,128,4,128]{3,1,0,2:T(8,128)(2,1)S(1)}, bf16[4,128,4,128]{3,1,0,2:T(8,128)(2,1)}, u32[]{:S(2)}) copy-start(bf16[4,128,4,128]{3,1,0,2:T(8,128)(2,1)} %get-tuple-element.109) | copy-start | bytes 1572868
  196.6 3.8 %copy-start.21 = (bf16[4,128,4,128]{3,1,0,2:T(8,128)(2,1)S(1)}, bf16[4,128,4,128]{3,1,0,2:T(8,128)(2,1)}, u32[]{:S(2)}) copy-start(bf16[4,128,4,128]{3,1,0,2:T(8,128)(2,1)} %get-tuple-element.104) | copy-start | bytes 1572868
  205.1 5.6 %copy-start.25 = (bf16[8,128,1,128]{3,1,0,2:T(8,128)(2,1)S(1)}, bf16[8,128,1,128]{3,1,0,2:T(8,128)(2,1)}, u32[]{:S(2)}) copy-start(bf16[8,128,1,128]{3,1,0,2:T(8,128)(2,1)} %get-tuple-element.110) | copy-start | bytes 786436
  210.7 7.3 %copy-start.5 = (bf16[4,512,1024]{1,2,0:T(8,128)(2,1)S(1)}, bf16[4,512,1024]{1,2,0:T(8,128)(2,1)}, u32[]{:S(2)}) copy-start(bf16[4,512,1024]{1,2,0:T(8,128)(2,1)} %fusion.22) | copy-start | bytes 12582916
  215.1 8.3 %copy-start.3 = (bf16[4,512,1024]{1,2,0:T(8,128)(2,1)}, bf16[4,512,1024]{1,2,0:T(8,128)(2,1)S(1)}, u32[]{:S(2)}) copy-start(bf16[4,512,1024]{1,2,0:T(8,128)(2,1)S(1)} %fusion.21) | copy-start | bytes 12582916
  215.1 5.2 %copy-start.20 = (bf16[4,128,4,128]{3,1,0,2:T(8,128)(2,1)S(1)}, bf16[4,128,4,128]{3,1,0,2:T(8,128)(2,1)}, u32[]{:S(2)}) copy-start(bf16[4,128,4,128]{3,1,0,2:T(8,128)(2,1)} %get-tuple-element.105) | copy-start | bytes 1572868
  215.1 5.2 %copy-start.24 = (bf16[8,128,1,128]{3,1,0,2:T(8,128)(2,1)S(1)}, bf16[8,128,1,128]{3,1,0,2:T(8,128)(2,1)}, u32[]{:S(2)}) copy-start(bf16[8,128,1,128]{3,1,0,2:T(8,128)(2,1)} %get-tuple-element.112) | copy-start | bytes 786436
  215.1 5.2 %copy-start.29 = (f32[512,1,4]{0,2,1:T(4,128)S(1)}, f32[512,1,4]{0,2,1:T(4,128)}, u32[]{:S(2)}) copy-start(f32[512,1,4]{0,2,1:T(4,128)} %reshape.626) | copy-start | bytes 24580
  220.3 3.0 copy-start.11
  223.4 7.4 %copy-start.6 = (bf16[4,512,1024]{1,2,0:T(8,128)(2,1)}, bf16[4,512,1024]{1,2,0:T(8,128)(2,1)S(1)}, u32[]{:S(2)}) copy-start(bf16[4,512,1024]{1,2,0:T(8,128)(2,1)S(1)} %fusion.23) | copy-start | bytes 12582916
  224.8 15.5 %collective-permute-start.2 = (bf16[2048,1,128]{2,0,1:T(8,128)(2,1)S(1)}, bf16[2048,1,128]{2,0,1:T(8,128)(2,1)S(1)}, u32[]{:S(2)}, u32[]{:S(2)}) collective-permute-start(bf16[2048,1,128]{2,0,1:T(8,128)(2,1)S(1)} %concatenate.38), channel_id=1, source_target_pairs={{16,0},{32,16},{48,32},{64,48},{80,64},{96,80},{112,96},{128,112},... | collective-permute-start | bytes 1572872 | tf_op jit(solution)/shard_map/ppermute | solution.py:10
  231.7 45.7 %copy-start.18 = (bf16[8,128,1,128]{3,1,0,2:T(8,128)(2,1)S(1)}, bf16[8,128,1,128]{3,1,0,2:T(8,128)(2,1)}, u32[]{:S(2)}) copy-start(bf16[8,128,1,128]{3,1,0,2:T(8,128)(2,1)} %get-tuple-element.115) | copy-start | bytes 786436
  231.7 22.9 %collective-permute-start.3 = (bf16[2048,1,128]{2,0,1:T(8,128)(2,1)}, bf16[2048,1,128]{2,0,1:T(8,128)(2,1)}, u32[]{:S(2)}, u32[]{:S(2)}) collective-permute-start(bf16[2048,1,128]{2,0,1:T(8,128)(2,1)} %concatenate.39), channel_id=1, source_target_pairs={{16,0},{32,16},{48,32},{64,48},{80,64},{96,80},{112,96},{128,112},... | collective-permute-start | bytes 1572872 | tf_op jit(solution)/shard_map/ppermute | solution.py:10
  241.4 29.6 %all-to-all-start.6 = ((f32[2048,1,128]{2,1,0:T(1,128)}), f32[2048,1,128]{2,1,0:T(1,128)S(1)}, u32[]{:S(2)}, u32[]{:S(2)}) async-start(f32[2048,1,128]{2,1,0:T(1,128)} %bitcast.468), calls=%async_computation.6 | async-start | bytes 2097152 | tf_op jit(solution)/shard_map/all_to_all | solution.py:105
  271.0 12.4 %copy-start.15 = (f32[2048,1,128]{2,1,0:T(1,128)}, f32[2048,1,128]{2,1,0:T(1,128)S(1)}, u32[]{:S(2)}) copy-start(f32[2048,1,128]{2,1,0:T(1,128)S(1)} %all-to-all-done.6) | copy-start | bytes 3145732
  271.0 22.9 %all-to-all-start.7 = ((f32[2048,1,128]{2,1,0:T(1,128)}), f32[2048,1,128]{2,1,0:T(1,128)}, u32[]{:S(2)}, u32[]{:S(2)}) async-start(f32[2048,1,128]{2,1,0:T(1,128)} %bitcast.467), calls=%async_computation.7 | async-start | bytes 2097152 | tf_op jit(solution)/shard_map/all_to_all | solution.py:106
  277.3 6.1 %copy-start.4 = (bf16[4,512,1024]{1,2,0:T(8,128)(2,1)S(1)}, bf16[4,512,1024]{1,2,0:T(8,128)(2,1)}, u32[]{:S(2)}) copy-start(bf16[4,512,1024]{1,2,0:T(8,128)(2,1)} %copy-done.3) | copy-start | bytes 12582916
  280.4 3.8 %copy-start.23 = (bf16[512,4,128]{0,2,1:T(8,128)(2,1)S(1)}, bf16[512,4,128]{0,2,1:T(8,128)(2,1)}, u32[]{:S(2)}) copy-start(bf16[512,4,128]{0,2,1:T(8,128)(2,1)} %fusion.58) | copy-start | bytes 1572868
  293.9 34.7 %all-to-all-start.5 = ((bf16[2048,4,128]{2,1,0:T(4,128)(2,1)}), bf16[2048,4,128]{2,1,0:T(4,128)(2,1)S(1)}, u32[]{:S(2)}, u32[]{:S(2)}) async-start(bf16[2048,4,128]{2,1,0:T(4,128)(2,1)} %copy.39), calls=%async_computation.5 | async-start | bytes 4194304 | tf_op jit(solution)/shard_map/all_to_all | solution.py:103
  (12 other events, 23.1 us)
where the time goes:
time: 338 us; the launch traced here: 331 us
  waiting for transfers between devices  149 us (44%)
  starting transfers between devices  66.3 us (20%)
  matrix products  51.4 us (15%)
  local copies, waits for them, and re-layouts  40.3 us (12%)
  other arithmetic  22.4 us (7%)
    ppermute x4, waiting for transfers between devices, shifted(): return lax.ppermute(block, axis, route)  37.3 us
    all_to_all x1, waiting for transfers between devices, heads_layout(): lax.all_to_all(outputs, 'head', split_axis=1, concat_axis=0, tiled=True)  25.2 us
    all_to_all x1, waiting for transfers between devices, heads_layout(): lax.all_to_all(queries, 'head', split_axis=1, concat_axis=0, tiled=True)  25.2 us
    all_to_all x1, waiting for transfers between devices, heads_layout(): lax.all_to_all(query_local, 'head', split_axis=0, concat_axis=1, tiled=True)  25.1 us
    unnamed x71, local copies, waits for them, and re-layouts  20.2 us
    dot_general x4, matrix products, heads_layout(): jnp.einsum('bkgd,wkd->kgbw', g_block, v_window, preferred_element_type=jn...  16.9 us
    all_to_all x1, waiting for transfers between devices, heads_layout(): lax.all_to_all(own_keys, 'head', split_axis=0, concat_axis=1, tiled=True)  14.3 us
    ppermute x4, starting transfers between devices, shifted(): return lax.ppermute(block, axis, route)  14.1 us
  transfers between devices with their start and end apart: 12, of which 10 were waited for; matrix products, arithmetic and copies ran while one was open for 15% of the time, Pallas kernels for 0%

commit v1 on v0

v1 whole, which is shorter than its diff:
```python
import functools
import math

import jax
import jax.numpy as jnp
from jax import lax
from jax.experimental import pallas as pl
from jax.experimental.pallas import tpu as pltpu
from jax.sharding import PartitionSpec as P

AXES = ("ctx", "head")
BLK = 128
NEG = -1e30
CHUNKS = 4
LANES = 256


def chip_shift(x, chips):
    n = lax.axis_size("ctx") * lax.axis_size("head")
    return lax.ppermute(x, AXES, [(i, (i + 2 * chips) % n) for i in range(n)])


def swap_cores(x):
    n = lax.axis_size("ctx") * lax.axis_size("head")
    return lax.ppermute(x, AXES, [(i, i ^ 1) for i in range(n)])


def chunk_kernel(
    scal, q_own, q_twin, g_own, g_twin, d_own, d_twin, start, kv_own, kv_a, kv_b,
    dq_own, dq_twin, dkv_own, dkv_a, dkv_b,
    qs, gs, ds_, kbuf, vbuf, ktr, dk, dv,
):
    core = scal[0]
    scale = HDSCALE
    rows = qs.shape[1]
    for slot, (q, g, d) in enumerate(((q_own, g_own, d_own), (q_twin, g_twin, d_twin))):
        qs[slot] = q[...].astype(jnp.float32).reshape(rows, BLK).astype(jnp.bfloat16)
        gs[slot] = g[...].astype(jnp.float32).reshape(rows, BLK).astype(jnp.bfloat16)
        ds_[slot] = d[...]
    for n, src in enumerate((kv_b, kv_a, kv_own)):
        kbuf[256 * n : 256 * (n + 1), :] = src[0]
        vbuf[256 * n : 256 * (n + 1), :] = src[1]
        ktr[:, 256 * n : 256 * (n + 1)] = src[0].T
    dk[...] = jnp.zeros_like(dk)
    dv[...] = jnp.zeros_like(dv)

    for rb in range(2):
        slot = jnp.where(core == rb, 0, 1)
        k0 = rb * BLK
        kwin = kbuf[k0 : k0 + 5 * BLK, :]
        vwin = vbuf[k0 : k0 + 5 * BLK, :]
        kt = ktr[:, k0 : k0 + 5 * BLK]

        def tile(lt, _):
            base = pl.multiple_of(lt * LANES, LANES)
            q_t = qs[slot, pl.ds(base, LANES), :]
            g_t = gs[slot, pl.ds(base, LANES), :]
            del_t = ds_[slot, :, pl.ds(base, LANES)]
            st = start[rb, :, pl.ds(base, LANES)]
            nt = (((1,), (1,)), ((), ()))
            s = lax.dot_general(kwin, q_t, nt, preferred_element_type=jnp.float32)
            u = lax.broadcasted_iota(jnp.int32, s.shape, 0)
            tok = 4 * BLK + ((base + lax.broadcasted_iota(jnp.int32, s.shape, 1)) >> 3)
            ok = (u >= st) & (u <= tok)
            s = jnp.where(ok, s * (scale * math.log2(math.e)), NEG)
            m = jnp.max(s, axis=0, keepdims=True)
            e = jnp.exp2(s - m)
            inv = 1.0 / jnp.sum(e, axis=0, keepdims=True)
            p = e * inv
            dp = lax.dot_general(vwin, g_t, nt, preferred_element_type=jnp.float32)
            dsc = (p * (dp - del_t)).astype(jnp.bfloat16)
            dv[k0 : k0 + 5 * BLK, :] += jnp.dot(
                p.astype(jnp.bfloat16), g_t, preferred_element_type=jnp.float32
            )
            dk[k0 : k0 + 5 * BLK, :] += jnp.dot(dsc, q_t, preferred_element_type=jnp.float32)
            dqt = jnp.dot(kt, dsc, preferred_element_type=jnp.float32)
            dqv = (dqt.T * scale).reshape(LANES // 8, 8, BLK).astype(jnp.bfloat16)
            tb = pl.multiple_of(lt * (LANES // 8), LANES // 8)

            @pl.when(slot == 0)
            def _():
                dq_own[pl.ds(tb, LANES // 8)] = dqv

            @pl.when(slot == 1)
            def _():
                dq_twin[pl.ds(tb, LANES // 8)] = dqv

            return 0

        lax.fori_loop(0, rows // LANES, tile, 0)
    for n, dst in enumerate((dkv_b, dkv_a, dkv_own)):
        dst[0] = (dk[256 * n : 256 * (n + 1), :] * scale).astype(dst.dtype)
        dst[1] = dv[256 * n : 256 * (n + 1), :].astype(dst.dtype)


HDSCALE = 128 ** (-0.5)


def chunk_call(core, h0, nh, q4, qt, g4, gt, d_own, d_twin, start, kv_own, kv_a, kv_b):
    rows = BLK * 8
    own = pl.BlockSpec((BLK, None, 8, BLK), lambda h, s: (0, 4 * s[0] + h0 + h, 0, 0))
    twin = pl.BlockSpec((BLK, None, 8, BLK), lambda h, s: (0, h0 + h, 0, 0))
    d_o = pl.BlockSpec((None, 1, rows), lambda h, s: (4 * s[0] + h0 + h, 0, 0))
    d_t = pl.BlockSpec((None, 1, rows), lambda h, s: (h0 + h, 0, 0))
    st = pl.BlockSpec((2, 1, rows), lambda h, s: (0, 0, 0))
    kvo = pl.BlockSpec((None, 2, 256, BLK), lambda h, s: (h0 + h, 0, 0, 0))
    kvc = pl.BlockSpec((None, 2, 256, BLK), lambda h, s: (h, 0, 0, 0))
    dqs = pl.BlockSpec((BLK, None, 8, BLK), lambda h, s: (0, h, 0, 0))
    return pl.pallas_call(
        chunk_kernel,
        grid_spec=pltpu.PrefetchScalarGridSpec(
            num_scalar_prefetch=1,
            grid=(nh,),
            in_specs=[own, twin, own, twin, d_o, d_t, st, kvo, kvc, kvc],
            out_specs=[dqs, dqs, kvc, kvc, kvc],
            scratch_shapes=[
                pltpu.VMEM((2, rows, BLK), jnp.bfloat16),
                pltpu.VMEM((2, rows, BLK), jnp.bfloat16),
                pltpu.VMEM((2, 1, rows), jnp.float32),
                pltpu.VMEM((768, BLK), jnp.bfloat16),
                pltpu.VMEM((768, BLK), jnp.bfloat16),
                pltpu.VMEM((BLK, 768), jnp.bfloat16),
                pltpu.VMEM((768, BLK), jnp.float32),
                pltpu.VMEM((768, BLK), jnp.float32),
            ],
        ),
        out_shape=[
            jax.ShapeDtypeStruct((BLK, nh, 8, BLK), jnp.bfloat16),
            jax.ShapeDtypeStruct((BLK, nh, 8, BLK), jnp.bfloat16),
            jax.ShapeDtypeStruct((nh, 2, 256, BLK), jnp.float32),
            jax.ShapeDtypeStruct((nh, 2, 256, BLK), jnp.bfloat16),
            jax.ShapeDtypeStruct((nh, 2, 256, BLK), jnp.bfloat16),
        ],
        compiler_params=pltpu.CompilerParams(vmem_limit_bytes=40 << 20),
        cost_estimate=pl.CostEstimate(
            flops=nh * 2 * 5 * 2 * rows * 640 * 128,
            bytes_accessed=nh * (6 * rows * 256 + 7 * 131072),
            transcendentals=nh * 2 * rows * 640,
        ),
        name="attention_chunk",
    )(core.reshape(1), q4, qt, g4, gt, d_own, d_twin, start, kv_own, kv_a, kv_b)


def shards(queries, keys, values, outputs, out_grad, segments):
    head = lax.axis_index("head")
    dev = lax.axis_index("ctx") * lax.axis_size("head") + head
    core = dev % 2
    chip = dev // 2
    nh = 4 // CHUNKS

    kvt = jnp.stack(
        [jnp.transpose(keys, (1, 0, 2)), jnp.transpose(values, (1, 0, 2))], axis=1
    )
    kv2 = kvt.reshape(2, 4, 2, BLK, BLK)
    mine = lax.dynamic_index_in_dim(kv2, core, 0, keepdims=False)
    other = swap_cores(lax.dynamic_index_in_dim(kv2, 1 - core, 0, keepdims=False))
    lo = jnp.where(core == 0, mine, other)
    hi = jnp.where(core == 0, other, mine)
    kvc = jnp.concatenate([lo, hi], axis=2)

    kv_a = [chip_shift(kvc[c * nh : (c + 1) * nh], 1) for c in range(CHUNKS)]
    kv_b = [chip_shift(kvc[c * nh : (c + 1) * nh], 2) for c in range(CHUNKS)]

    q4 = queries.reshape(BLK, 8, 8, BLK)
    g4 = out_grad.reshape(BLK, 8, 8, BLK)
    qt = swap_cores(lax.dynamic_slice_in_dim(q4, 4 * (1 - core), 4, 1))
    gt = swap_cores(lax.dynamic_slice_in_dim(g4, 4 * (1 - core), 4, 1))
    delta = jnp.sum(outputs.astype(jnp.float32) * out_grad.astype(jnp.float32), axis=-1)
    delta = jnp.transpose(delta.reshape(BLK, 8, 8), (1, 0, 2)).reshape(8, 1, BLK * 8)
    d_twin = swap_cores(lax.dynamic_slice_in_dim(delta, 4 * (1 - core), 4, 0))

    seg_pad = jnp.concatenate([jnp.full((512,), -1, jnp.int32), segments])
    seg_w = lax.dynamic_slice_in_dim(seg_pad, chip * 256, 768, 0)
    first = jnp.sum((seg_w[None, :] < seg_w[512:, None]).astype(jnp.int32), axis=1)
    first = first.reshape(2, BLK) - jnp.array([[0], [BLK]], jnp.int32)
    start = jnp.broadcast_to(first[:, :, None], (2, BLK, 8)).reshape(2, 1, BLK * 8)

    dq_own, dq_twin, own, back_a, back_b = [], [], [], [], []
    for c in range(CHUNKS):
        o, t, dkv_o, dkv_a, dkv_b = chunk_call(
            core, c * nh, nh, q4, qt, g4, gt, delta, d_twin, start, kvc, kv_a[c], kv_b[c]
        )
        dq_own.append(o)
        dq_twin.append(swap_cores(t))
        own.append(dkv_o)
        back_b.append(chip_shift(dkv_b, -2))
        back_a.append(chip_shift(dkv_a, -1))
    o = jnp.concatenate(dq_own, axis=1)
    t = jnp.concatenate(dq_twin, axis=1)
    dq = jnp.concatenate(
        [jnp.where(core == 0, o, t), jnp.where(core == 0, t, o)], axis=1
    ).reshape(BLK, 64, BLK)

    total = jnp.concatenate(
        [
            (a + b.astype(jnp.float32) + c.astype(jnp.float32)).astype(jnp.bfloat16)
            for a, b, c in zip(own, back_a, back_b)
        ],
        axis=0,
    ).reshape(4, 2, 2, BLK, BLK)
    keep = lax.dynamic_index_in_dim(total, core, 2, keepdims=False)
    got = swap_cores(lax.dynamic_index_in_dim(total, 1 - core, 2, keepdims=False))
    full = jnp.concatenate(
        [jnp.where(core == 0, keep, got), jnp.where(core == 0, got, keep)], axis=0
    )
    dkeys = jnp.transpose(full[:, 0], (1, 0, 2))
    dvals = jnp.transpose(full[:, 1], (1, 0, 2))
    return dq, dkeys, dvals


def solution(mesh):
    spec = P(AXES, None, None)
    return jax.shard_map(
        shards,
        mesh=mesh,
        in_specs=(spec, spec, spec, spec, spec, P()),
        out_specs=(spec, spec, spec),
        check_vma=False,
    )
```

time: 338 us -> 110 us (0.33)
  the two profiles are of different devices: /device:TPU:121 before, /device:TPU:17 now
where the time goes in v1:
time: 110 us
  starting transfers between devices  46.9 us (43%)
  Pallas kernels  40.3 us (37%)
  local copies, waits for them, and re-layouts  15.2 us (14%)
  other arithmetic  6.54 us (6%)
    pallas_call x4, Pallas kernels, chunk_call(): pl.pallas_call(chunk_kernel, grid_spec=pltpu.PrefetchScalarGridSpec(num_s...  40.3 us
    ppermute x16, starting transfers between devices, chip_shift(): return lax.ppermute(x, AXES, [(i, (i + 2 * chips) % n) for i in range(n)])  33.1 us
    ppermute x9, starting transfers between devices, swap_cores(): return lax.ppermute(x, AXES, [(i, i ^ 1) for i in range(n)])  13.9 us
    unnamed x23, local copies, waits for them, and re-layouts  4.85 us
    dynamic_slice x1, local copies, waits for them, and re-layouts, shards(): qt = swap_cores(lax.dynamic_slice_in_dim(q4, 4 * (1 - core), 4, 1))  2.43 us
  transfers between devices with their start and end apart: 25, of which 0 were waited for; matrix products, arithmetic and copies ran while one was open for 14% of the time, Pallas kernels for 37%

profile of v1, /device:TPU:17, one launch (start us, length us, event | category | flops | bytes accessed | tf_op | source)
XLA Modules:
  0.0 110.1 jit_solution(6538543050172857963)
XLA Ops:
  0.7 1.1 %copy_dynamic-update-slice_fusion.1 = bf16[2,4,2,128,128]{4,3,2,1,0:T(8,128)(2,1)S(1)} fusion(bf16[2,4,1,128,128]{4,1,0,3,2:T(4,128)(2,1)} %bitcast.51), kind=kLoop, calls=%fused_computation.26 | loop fusion | bytes 524288
  1.8 1.0 copy_dynamic-update-slice_fusion
  4.3 2.4 %constant_dynamic-slice_fusion.2 = bf16[128,4,8,128]{3,2,1,0:T(8,128)(2,1)} fusion(bf16[128,8,8,128]{3,2,1,0:T(8,128)(2,1)} %bitcast.44, s32[]{:T(128)S(6)} %select_n.63), kind=kLoop, calls=%fused_computation.48 | loop fusion | bytes 2097156 | tf_op jit(solution)/shard_map/dynamic_slice | solution.py:166
  6.8 1.1 constant_dynamic-slice_fusion.1
  8.3 1.2 %multiply_reduce_fusion = f32[128,64]{1,0:T(8,128)S(1)} fusion(bf16[128,64,128]{2,1,0:T(8,128)(2,1)S(1)} %copy-done, bf16[128,64,128]{2,1,0:T(8,128)(2,1)S(1)} %copy-done.4), kind=kLoop, calls=%fused_computation | loop fusion | flops 4186112 | bytes 4227072 | tf_op jit(solution)/shard_map/reduce_sum | solution.py:168
  9.5 1.0 copy.50
  10.5 1.3 %reshape.73.d_own = f32[8,1,1024]{2,1,0:T(1,128)S(1)} reshape(f32[8,128,8]{2,1,0:T(8,128)} %copy.50) | data formatting | bytes 65536 | tf_op jit(solution)/shard_map/reshape | solution.py:169
  13.1 1.0 bitcast_select_fusion.3
  14.1 0.9 fusion.6
  15.0 1.0 collective-permute-start.4
  16.0 2.8 %collective-permute-start.5 = (bf16[1,2,256,128]{3,2,1,0:T(8,128)(2,1)}, bf16[1,2,256,128]{3,2,1,0:T(8,128)(2,1)S(1)}, u32[]{:S(2)}, u32[]{:S(2)}) collective-permute-start(bf16[1,2,256,128]{3,2,1,0:T(8,128)(2,1)} %get-tuple-element.64), channel_id=1, source_target_pairs={{0,4},{1,5},{2,6},{3,7},{4,8},{5,9},{6,10},{7,11},{8,12},{9,13},{1... | collective-permute-start | bytes 393224 | tf_op jit(solution)/shard_map/ppermute | solution.py:20
  19.6 1.0 reshape.74.start
  20.7 1.1 pad_maximum_fusion.kv_own
  21.7 2.0 %collective-permute-start.6 = (bf16[1,2,256,128]{3,2,1,0:T(8,128)(2,1)}, bf16[1,2,256,128]{3,2,1,0:T(8,128)(2,1)S(1)}, u32[]{:S(2)}, u32[]{:S(2)}) collective-permute-start(bf16[1,2,256,128]{3,2,1,0:T(8,128)(2,1)} %get-tuple-element.65), channel_id=1, source_target_pairs={{0,2},{1,3},{2,4},{3,5},{4,6},{5,7},{6,8},{7,9},{8,10},{9,11},{10,... | collective-permute-start | bytes 393224 | tf_op jit(solution)/shard_map/ppermute | solution.py:20
  23.7 2.4 %collective-permute-start.7 = (bf16[1,2,256,128]{3,2,1,0:T(8,128)(2,1)}, bf16[1,2,256,128]{3,2,1,0:T(8,128)(2,1)S(1)}, u32[]{:S(2)}, u32[]{:S(2)}) collective-permute-start(bf16[1,2,256,128]{3,2,1,0:T(8,128)(2,1)} %get-tuple-element.65), channel_id=1, source_target_pairs={{0,4},{1,5},{2,6},{3,7},{4,8},{5,9},{6,10},{7,11},{8,12},{9,13},{1... | collective-permute-start | bytes 393224 | tf_op jit(solution)/shard_map/ppermute | solution.py:20
  26.1 3.5 %collective-permute-start.9 = (bf16[1,2,256,128]{3,2,1,0:T(8,128)(2,1)}, bf16[1,2,256,128]{3,2,1,0:T(8,128)(2,1)S(1)}, u32[]{:S(2)}, u32[]{:S(2)}) collective-permute-start(bf16[1,2,256,128]{3,2,1,0:T(8,128)(2,1)} %get-tuple-element.66), channel_id=1, source_target_pairs={{0,4},{1,5},{2,6},{3,7},{4,8},{5,9},{6,10},{7,11},{8,12},{9,13},{1... | collective-permute-start | bytes 393224 | tf_op jit(solution)/shard_map/ppermute | solution.py:20
  30.2 1.6 %copy-done.1 = bf16[128,64,128]{2,1,0:T(8,128)(2,1)S(1)} copy-done((bf16[128,64,128]{2,1,0:T(8,128)(2,1)S(1)}, bf16[128,64,128]{2,1,0:T(8,128)(2,1)}, u32[]{:S(2)}) %copy-start.1) | copy-done | bytes 2097176
  31.8 10.1 %attention_chunk.4 = (bf16[128,1,8,128]{3,2,1,0:T(8,128)(2,1)S(1)}, bf16[128,1,8,128]{3,2,1,0:T(8,128)(2,1)S(1)}, f32[1,2,256,128]{3,2,1,0:T(8,128)S(1)}, bf16[1...) custom-call(s32[1]{0:T(128)} %bitcast.scal, bf16[128,8,8,128]{3,2,1,0:T(8,128)(2,1)S(1)} %bitcast.45, ...), custom_call_target="tpu_custom_call" | custom-call | flops 1677721600 | bytes 2490368 | tf_op jit(solution)/shard_map/attention_chunk/pallas_call | solution.py:109
  41.9 1.4 %collective-permute-start.11 = (bf16[1,2,256,128]{3,2,1,0:T(8,128)(2,1)S(1)}, bf16[1,2,256,128]{3,2,1,0:T(8,128)(2,1)S(1)}, u32[]{:S(2)}, u32[]{:S(2)}) collective-permute-start(bf16[1,2,256,128]{3,2,1,0:T(8,128)(2,1)S(1)} %copy-done.6), channel_id=1, source_target_pairs={{0,4},{1,5},{2,6},{3,7},{4,8},{5,9},{6,10},{7,11},{8,12},{9,13},{1... | collective-permute-start | bytes 393224 | tf_op jit(solution)/shard_map/ppermute | solution.py:20
  43.7 10.1 %attention_chunk.5 = (bf16[128,1,8,128]{3,2,1,0:T(8,128)(2,1)S(1)}, bf16[128,1,8,128]{3,2,1,0:T(8,128)(2,1)S(1)}, f32[1,2,256,128]{3,2,1,0:T(8,128)S(1)}, bf16[1...) custom-call(s32[1]{0:T(128)} %bitcast.scal, bf16[128,8,8,128]{3,2,1,0:T(8,128)(2,1)S(1)} %bitcast.46, ...), custom_call_target="tpu_custom_call" | custom-call | flops 1677721600 | bytes 2490368 | tf_op jit(solution)/shard_map/attention_chunk/pallas_call | solution.py:109
  53.8 7.8 %collective-permute-start.17 = (bf16[1,2,256,128]{3,2,1,0:T(8,128)(2,1)S(1)}, bf16[1,2,256,128]{3,2,1,0:T(8,128)(2,1)S(1)}, u32[]{:S(2)}, u32[]{:S(2)}) collective-permute-start(bf16[1,2,256,128]{3,2,1,0:T(8,128)(2,1)S(1)} %get-tuple-element.33), channel_id=1, source_target_pairs={{0,252},{1,253},{2,254},{3,255},{4,0},{5,1},{6,2},{7,3},{8,4},{9,5... | collective-permute-start | bytes 393224 | tf_op jit(solution)/shard_map/ppermute | solution.py:20
  61.9 10.1 %attention_chunk.6 = (bf16[128,1,8,128]{3,2,1,0:T(8,128)(2,1)S(1)}, bf16[128,1,8,128]{3,2,1,0:T(8,128)(2,1)S(1)}, f32[1,2,256,128]{3,2,1,0:T(8,128)S(1)}, bf16[1...) custom-call(s32[1]{0:T(128)} %bitcast.scal, bf16[128,8,8,128]{3,2,1,0:T(8,128)(2,1)S(1)} %bitcast.47, ...), custom_call_target="tpu_custom_call" | custom-call | flops 1677721600 | bytes 2490368 | tf_op jit(solution)/shard_map/attention_chunk/pallas_call | solution.py:109
  72.1 4.2 %collective-permute-start.19 = (bf16[1,2,256,128]{3,2,1,0:T(8,128)(2,1)S(1)}, bf16[1,2,256,128]{3,2,1,0:T(8,128)(2,1)S(1)}, u32[]{:S(2)}, u32[]{:S(2)}) collective-permute-start(bf16[1,2,256,128]{3,2,1,0:T(8,128)(2,1)S(1)} %get-tuple-element.36), channel_id=1, source_target_pairs={{0,252},{1,253},{2,254},{3,255},{4,0},{5,1},{6,2},{7,3},{8,4},{9,5... | collective-permute-start | bytes 393224 | tf_op jit(solution)/shard_map/ppermute | solution.py:20
  76.3 2.6 %collective-permute-start.20 = (bf16[1,2,256,128]{3,2,1,0:T(8,128)(2,1)S(1)}, bf16[1,2,256,128]{3,2,1,0:T(8,128)(2,1)S(1)}, u32[]{:S(2)}, u32[]{:S(2)}) collective-permute-start(bf16[1,2,256,128]{3,2,1,0:T(8,128)(2,1)S(1)} %get-tuple-element.38), channel_id=1, source_target_pairs={{0,254},{1,255},{2,0},{3,1},{4,2},{5,3},{6,4},{7,5},{8,6},{9,7},{1... | collective-permute-start | bytes 393224 | tf_op jit(solution)/shard_map/ppermute | solution.py:20
  78.9 10.1 %attention_chunk.7 = (bf16[128,1,8,128]{3,2,1,0:T(8,128)(2,1)S(1)}, bf16[128,1,8,128]{3,2,1,0:T(8,128)(2,1)S(1)}, f32[1,2,256,128]{3,2,1,0:T(8,128)S(1)}, bf16[1...) custom-call(s32[1]{0:T(128)} %bitcast.scal, bf16[128,8,8,128]{3,2,1,0:T(8,128)(2,1)S(1)} %bitcast.48, ...), custom_call_target="tpu_custom_call" | custom-call | flops 1677721600 | bytes 2490368 | tf_op jit(solution)/shard_map/attention_chunk/pallas_call | solution.py:109
  89.1 1.7 %collective-permute-start.21 = (bf16[1,2,256,128]{3,2,1,0:T(8,128)(2,1)S(1)}, bf16[1,2,256,128]{3,2,1,0:T(8,128)(2,1)S(1)}, u32[]{:S(2)}, u32[]{:S(2)}) collective-permute-start(bf16[1,2,256,128]{3,2,1,0:T(8,128)(2,1)S(1)} %get-tuple-element.39), channel_id=1, source_target_pairs={{0,252},{1,253},{2,254},{3,255},{4,0},{5,1},{6,2},{7,3},{8,4},{9,5... | collective-permute-start | bytes 393224 | tf_op jit(solution)/shard_map/ppermute | solution.py:20
  91.7 1.6 %collective-permute-start.23 = (bf16[1,2,256,128]{3,2,1,0:T(8,128)(2,1)S(1)}, bf16[1,2,256,128]{3,2,1,0:T(8,128)(2,1)S(1)}, u32[]{:S(2)}, u32[]{:S(2)}) collective-permute-start(bf16[1,2,256,128]{3,2,1,0:T(8,128)(2,1)S(1)} %get-tuple-element.42), channel_id=1, source_target_pairs={{0,252},{1,253},{2,254},{3,255},{4,0},{5,1},{6,2},{7,3},{8,4},{9,5... | collective-permute-start | bytes 393224 | tf_op jit(solution)/shard_map/ppermute | solution.py:20
  93.3 5.2 %collective-permute-start.13 = (bf16[128,1,8,128]{3,2,1,0:T(8,128)(2,1)S(1)}, bf16[128,1,8,128]{3,2,1,0:T(8,128)(2,1)S(1)}, u32[]{:S(2)}, u32[]{:S(2)}) collective-permute-start(bf16[128,1,8,128]{3,2,1,0:T(8,128)(2,1)S(1)} %get-tuple-element.28), channel_id=1, source_target_pairs={{0,1},{1,0},{2,3},{3,2},{4,5},{5,4},{6,7},{7,6},{8,9},{9,8},{10,11... | collective-permute-start | bytes 786440 | tf_op jit(solution)/shard_map/ppermute | solution.py:25
  98.7 3.3 %collective-permute-start.14 = (bf16[128,1,8,128]{3,2,1,0:T(8,128)(2,1)S(1)}, bf16[128,1,8,128]{3,2,1,0:T(8,128)(2,1)S(1)}, u32[]{:S(2)}, u32[]{:S(2)}) collective-permute-start(bf16[128,1,8,128]{3,2,1,0:T(8,128)(2,1)S(1)} %get-tuple-element.29), channel_id=1, source_target_pairs={{0,1},{1,0},{2,3},{3,2},{4,5},{5,4},{6,7},{7,6},{8,9},{9,8},{10,11... | collective-permute-start | bytes 786440 | tf_op jit(solution)/shard_map/ppermute | solution.py:25
  102.3 3.8 %collective-permute-start.24 = (bf16[4,2,128,128]{3,2,1,0:T(8,128)(2,1)S(1)}, bf16[4,2,128,128]{3,2,1,0:T(8,128)(2,1)S(1)}, u32[]{:S(2)}, u32[]{:S(2)}) collective-permute-start(bf16[4,2,128,128]{3,2,1,0:T(8,128)(2,1)S(1)} %dynamic-slice_bitcast_fusion), channel_id=1, source_target_pairs={{0,1},{1,0},{2,3},{3,2},{4,5},{5,4},{6,7},{7,6},{8,9},{9,8},{10,11... | collective-permute-start | bytes 786440 | tf_op jit(solution)/shard_map/ppermute | solution.py:25
  106.7 1.5 %maximum_bitcast_fusion = bf16[128,64,128]{2,1,0:T(8,128)(2,1)} fusion(bf16[128,4,8,128]{3,2,1,0:T(8,128)(2,1)S(1)} %get-tuple-element.56, bf16[128,4,8,128]{3,2,1,0:T(8,128)(2,1)S(1)} %get-tuple-element.55), kind=kLoop, calls=%fused_computation.1 | loop fusion | flops 1048576 | bytes 4194304 | tf_op jit(solution)/shard_map/reshape | solution.py:192
  108.3 0.9 copy.64
  (76 shorter events, 8.5 us)
Async XLA Ops:
  0.6 6.2 %copy-start = (bf16[128,64,128]{2,1,0:T(8,128)(2,1)S(1)}, bf16[128,64,128]{2,1,0:T(8,128)(2,1)}, u32[]{:S(2)}) copy-start(bf16[128,64,128]{2,1,0:T(8,128)(2,1)} %param.11) | copy-start | bytes 6291460
  2.8 1.5 %copy-start.5 = (bf16[2,4,2,128,128]{4,3,2,1,0:T(8,128)(2,1)}, bf16[2,4,2,128,128]{4,3,2,1,0:T(8,128)(2,1)S(1)}, u32[]{:S(2)}) copy-start(bf16[2,4,2,128,128]{4,3,2,1,0:T(8,128)(2,1)S(1)} %copy_dynamic-update-slice_fusion) | copy-start | bytes 1572868
  3.6 9.5 %collective-permute-start.3 = (bf16[4,2,128,128]{3,2,1,0:T(8,128)(2,1)}, bf16[4,2,128,128]{3,2,1,0:T(8,128)(2,1)S(1)}, u32[]{:S(2)}, u32[]{:S(2)}) collective-permute-start(bf16[4,2,128,128]{3,2,1,0:T(8,128)(2,1)} %dynamic-slice_bitcast_fusion.1), channel_id=1, source_target_pairs={{0,1},{1,0},{2,3},{3,2},{4,5},{5,4},{6,7},{7,6},{8,9},{9,8},{10,11... | collective-permute-start | bytes 786440 | tf_op jit(solution)/shard_map/ppermute | solution.py:25
  4.3 4.0 %copy-start.4 = (bf16[128,64,128]{2,1,0:T(8,128)(2,1)S(1)}, bf16[128,64,128]{2,1,0:T(8,128)(2,1)}, u32[]{:S(2)}) copy-start(bf16[128,64,128]{2,1,0:T(8,128)(2,1)} %param.10) | copy-start | bytes 6291460
  6.7 19.4 %collective-permute-start = (bf16[128,4,8,128]{3,2,1,0:T(8,128)(2,1)}, bf16[128,4,8,128]{3,2,1,0:T(8,128)(2,1)S(1)}, u32[]{:S(2)}, u32[]{:S(2)}) collective-permute-start(bf16[128,4,8,128]{3,2,1,0:T(8,128)(2,1)} %constant_dynamic-slice_fusion.2), channel_id=1, source_target_pairs={{0,1},{1,0},{2,3},{3,2},{4,5},{5,4},{6,7},{7,6},{8,9},{9,8},{10,11... | collective-permute-start | bytes 3145736 | tf_op jit(solution)/shard_map/ppermute | solution.py:25
  7.9 21.7 %collective-permute-start.1 = (bf16[128,4,8,128]{3,2,1,0:T(8,128)(2,1)}, bf16[128,4,8,128]{3,2,1,0:T(8,128)(2,1)}, u32[]{:S(2)}, u32[]{:S(2)}) collective-permute-start(bf16[128,4,8,128]{3,2,1,0:T(8,128)(2,1)} %constant_dynamic-slice_fusion.1), channel_id=1, source_target_pairs={{0,1},{1,0},{2,3},{3,2},{4,5},{5,4},{6,7},{7,6},{8,9},{9,8},{10,11... | collective-permute-start | bytes 3145736 | tf_op jit(solution)/shard_map/ppermute | solution.py:25
  11.9 9.8 %collective-permute-start.2 = (f32[4,1,1024]{2,1,0:T(1,128)S(1)}, f32[4,1,1024]{2,1,0:T(1,128)S(1)}, u32[]{:S(2)}, u32[]{:S(2)}) collective-permute-start(f32[4,1,1024]{2,1,0:T(1,128)S(1)} %constant_dynamic-slice_fusion), channel_id=1, source_target_pairs={{0,1},{1,0},{2,3},{3,2},{4,5},{5,4},{6,7},{7,6},{8,9},{9,8},{10,11... | collective-permute-start | bytes 49160 | tf_op jit(solution)/shard_map/ppermute | solution.py:25
  14.1 4.8 %copy-start.2 = (bf16[4,2,128,128]{3,2,1,0:T(8,128)(2,1)}, bf16[4,2,128,128]{3,2,1,0:T(8,128)(2,1)S(1)}, u32[]{:S(2)}) copy-start(bf16[4,2,128,128]{3,2,1,0:T(8,128)(2,1)S(1)} %get-tuple-element.59) | copy-start | bytes 786436
  14.1 4.8 %copy-start.3 = (bf16[4,2,128,128]{3,2,1,0:T(8,128)(2,1)}, bf16[4,2,128,128]{3,2,1,0:T(8,128)(2,1)S(1)}, u32[]{:S(2)}) copy-start(bf16[4,2,128,128]{3,2,1,0:T(8,128)(2,1)S(1)} %get-tuple-element.60) | copy-start | bytes 786436
  15.0 8.7 %collective-permute-start.4 = (bf16[1,2,256,128]{3,2,1,0:T(8,128)(2,1)}, bf16[1,2,256,128]{3,2,1,0:T(8,128)(2,1)S(1)}, u32[]{:S(2)}, u32[]{:S(2)}) collective-permute-start(bf16[1,2,256,128]{3,2,1,0:T(8,128)(2,1)} %get-tuple-element.64), channel_id=1, source_target_pairs={{0,2},{1,3},{2,4},{3,5},{4,6},{5,7},{6,8},{7,9},{8,10},{9,11},{10,... | collective-permute-start | bytes 393224 | tf_op jit(solution)/shard_map/ppermute | solution.py:20
  16.0 10.1 %collective-permute-start.5 = (bf16[1,2,256,128]{3,2,1,0:T(8,128)(2,1)}, bf16[1,2,256,128]{3,2,1,0:T(8,128)(2,1)S(1)}, u32[]{:S(2)}, u32[]{:S(2)}) collective-permute-start(bf16[1,2,256,128]{3,2,1,0:T(8,128)(2,1)} %get-tuple-element.64), channel_id=1, source_target_pairs={{0,4},{1,5},{2,6},{3,7},{4,8},{5,9},{6,10},{7,11},{8,12},{9,13},{1... | collective-permute-start | bytes 393224 | tf_op jit(solution)/shard_map/ppermute | solution.py:20
  21.7 20.1 %collective-permute-start.6 = (bf16[1,2,256,128]{3,2,1,0:T(8,128)(2,1)}, bf16[1,2,256,128]{3,2,1,0:T(8,128)(2,1)S(1)}, u32[]{:S(2)}, u32[]{:S(2)}) collective-permute-start(bf16[1,2,256,128]{3,2,1,0:T(8,128)(2,1)} %get-tuple-element.65), channel_id=1, source_target_pairs={{0,2},{1,3},{2,4},{3,5},{4,6},{5,7},{6,8},{7,9},{8,10},{9,11},{10,... | collective-permute-start | bytes 393224 | tf_op jit(solution)/shard_map/ppermute | solution.py:20
  23.7 19.5 %collective-permute-start.7 = (bf16[1,2,256,128]{3,2,1,0:T(8,128)(2,1)}, bf16[1,2,256,128]{3,2,1,0:T(8,128)(2,1)S(1)}, u32[]{:S(2)}, u32[]{:S(2)}) collective-permute-start(bf16[1,2,256,128]{3,2,1,0:T(8,128)(2,1)} %get-tuple-element.65), channel_id=1, source_target_pairs={{0,4},{1,5},{2,6},{3,7},{4,8},{5,9},{6,10},{7,11},{8,12},{9,13},{1... | collective-permute-start | bytes 393224 | tf_op jit(solution)/shard_map/ppermute | solution.py:20
  26.1 27.7 %collective-permute-start.8 = (bf16[1,2,256,128]{3,2,1,0:T(8,128)(2,1)}, bf16[1,2,256,128]{3,2,1,0:T(8,128)(2,1)S(1)}, u32[]{:S(2)}, u32[]{:S(2)}) collective-permute-start(bf16[1,2,256,128]{3,2,1,0:T(8,128)(2,1)} %get-tuple-element.66), channel_id=1, source_target_pairs={{0,2},{1,3},{2,4},{3,5},{4,6},{5,7},{6,8},{7,9},{8,10},{9,11},{10,... | collective-permute-start | bytes 393224 | tf_op jit(solution)/shard_map/ppermute | solution.py:20
  26.1 35.5 %collective-permute-start.9 = (bf16[1,2,256,128]{3,2,1,0:T(8,128)(2,1)}, bf16[1,2,256,128]{3,2,1,0:T(8,128)(2,1)S(1)}, u32[]{:S(2)}, u32[]{:S(2)}) collective-permute-start(bf16[1,2,256,128]{3,2,1,0:T(8,128)(2,1)} %get-tuple-element.66), channel_id=1, source_target_pairs={{0,4},{1,5},{2,6},{3,7},{4,8},{5,9},{6,10},{7,11},{8,12},{9,13},{1... | collective-permute-start | bytes 393224 | tf_op jit(solution)/shard_map/ppermute | solution.py:20
  29.6 42.5 %collective-permute-start.10 = (bf16[1,2,256,128]{3,2,1,0:T(8,128)(2,1)}, bf16[1,2,256,128]{3,2,1,0:T(8,128)(2,1)S(1)}, u32[]{:S(2)}, u32[]{:S(2)}) collective-permute-start(bf16[1,2,256,128]{3,2,1,0:T(8,128)(2,1)} %get-tuple-element.63), channel_id=1, source_target_pairs={{0,2},{1,3},{2,4},{3,5},{4,6},{5,7},{6,8},{7,9},{8,10},{9,11},{10,... | collective-permute-start | bytes 393224 | tf_op jit(solution)/shard_map/ppermute | solution.py:20
  30.2 1.6 %copy-start.1 = (bf16[128,64,128]{2,1,0:T(8,128)(2,1)S(1)}, bf16[128,64,128]{2,1,0:T(8,128)(2,1)}, u32[]{:S(2)}) copy-start(bf16[128,64,128]{2,1,0:T(8,128)(2,1)} %param.7) | copy-start | bytes 6291460
  31.8 10.1 %copy-start.6 = (bf16[1,2,256,128]{3,2,1,0:T(8,128)(2,1)S(1)}, bf16[1,2,256,128]{3,2,1,0:T(8,128)(2,1)}, u32[]{:S(2)}) copy-start(bf16[1,2,256,128]{3,2,1,0:T(8,128)(2,1)} %get-tuple-element.63) | copy-start | bytes 393220
  41.9 34.4 %collective-permute-start.11 = (bf16[1,2,256,128]{3,2,1,0:T(8,128)(2,1)S(1)}, bf16[1,2,256,128]{3,2,1,0:T(8,128)(2,1)S(1)}, u32[]{:S(2)}, u32[]{:S(2)}) collective-permute-start(bf16[1,2,256,128]{3,2,1,0:T(8,128)(2,1)S(1)} %copy-done.6), channel_id=1, source_target_pairs={{0,4},{1,5},{2,6},{3,7},{4,8},{5,9},{6,10},{7,11},{8,12},{9,13},{1... | collective-permute-start | bytes 393224 | tf_op jit(solution)/shard_map/ppermute | solution.py:20
  43.3 45.9 %collective-permute-start.16 = (bf16[1,2,256,128]{3,2,1,0:T(8,128)(2,1)S(1)}, bf16[1,2,256,128]{3,2,1,0:T(8,128)(2,1)S(1)}, u32[]{:S(2)}, u32[]{:S(2)}) collective-permute-start(bf16[1,2,256,128]{3,2,1,0:T(8,128)(2,1)S(1)} %get-tuple-element.32), channel_id=1, source_target_pairs={{0,254},{1,255},{2,0},{3,1},{4,2},{5,3},{6,4},{7,5},{8,6},{9,7},{1... | collective-permute-start | bytes 393224 | tf_op jit(solution)/shard_map/ppermute | solution.py:20
  53.8 37.1 %collective-permute-start.17 = (bf16[1,2,256,128]{3,2,1,0:T(8,128)(2,1)S(1)}, bf16[1,2,256,128]{3,2,1,0:T(8,128)(2,1)S(1)}, u32[]{:S(2)}, u32[]{:S(2)}) collective-permute-start(bf16[1,2,256,128]{3,2,1,0:T(8,128)(2,1)S(1)} %get-tuple-element.33), channel_id=1, source_target_pairs={{0,252},{1,253},{2,254},{3,255},{4,0},{5,1},{6,2},{7,3},{8,4},{9,5... | collective-permute-start | bytes 393224 | tf_op jit(solution)/shard_map/ppermute | solution.py:20
  61.6 30.1 %collective-permute-start.18 = (bf16[1,2,256,128]{3,2,1,0:T(8,128)(2,1)S(1)}, bf16[1,2,256,128]{3,2,1,0:T(8,128)(2,1)S(1)}, u32[]{:S(2)}, u32[]{:S(2)}) collective-permute-start(bf16[1,2,256,128]{3,2,1,0:T(8,128)(2,1)S(1)} %get-tuple-element.35), channel_id=1, source_target_pairs={{0,254},{1,255},{2,0},{3,1},{4,2},{5,3},{6,4},{7,5},{8,6},{9,7},{1... | collective-permute-start | bytes 393224 | tf_op jit(solution)/shard_map/ppermute | solution.py:20
  72.1 21.2 %collective-permute-start.19 = (bf16[1,2,256,128]{3,2,1,0:T(8,128)(2,1)S(1)}, bf16[1,2,256,128]{3,2,1,0:T(8,128)(2,1)S(1)}, u32[]{:S(2)}, u32[]{:S(2)}) collective-permute-start(bf16[1,2,256,128]{3,2,1,0:T(8,128)(2,1)S(1)} %get-tuple-element.36), channel_id=1, source_target_pairs={{0,252},{1,253},{2,254},{3,255},{4,0},{5,1},{6,2},{7,3},{8,4},{9,5... | collective-permute-start | bytes 393224 | tf_op jit(solution)/shard_map/ppermute | solution.py:20
  76.3 22.3 %collective-permute-start.20 = (bf16[1,2,256,128]{3,2,1,0:T(8,128)(2,1)S(1)}, bf16[1,2,256,128]{3,2,1,0:T(8,128)(2,1)S(1)}, u32[]{:S(2)}, u32[]{:S(2)}) collective-permute-start(bf16[1,2,256,128]{3,2,1,0:T(8,128)(2,1)S(1)} %get-tuple-element.38), channel_id=1, source_target_pairs={{0,254},{1,255},{2,0},{3,1},{4,2},{5,3},{6,4},{7,5},{8,6},{9,7},{1... | collective-permute-start | bytes 393224 | tf_op jit(solution)/shard_map/ppermute | solution.py:20
  89.1 9.6 %collective-permute-start.21 = (bf16[1,2,256,128]{3,2,1,0:T(8,128)(2,1)S(1)}, bf16[1,2,256,128]{3,2,1,0:T(8,128)(2,1)S(1)}, u32[]{:S(2)}, u32[]{:S(2)}) collective-permute-start(bf16[1,2,256,128]{3,2,1,0:T(8,128)(2,1)S(1)} %get-tuple-element.39), channel_id=1, source_target_pairs={{0,252},{1,253},{2,254},{3,255},{4,0},{5,1},{6,2},{7,3},{8,4},{9,5... | collective-permute-start | bytes 393224 | tf_op jit(solution)/shard_map/ppermute | solution.py:20
  90.9 11.2 %collective-permute-start.22 = (bf16[1,2,256,128]{3,2,1,0:T(8,128)(2,1)S(1)}, bf16[1,2,256,128]{3,2,1,0:T(8,128)(2,1)S(1)}, u32[]{:S(2)}, u32[]{:S(2)}) collective-permute-start(bf16[1,2,256,128]{3,2,1,0:T(8,128)(2,1)S(1)} %get-tuple-element.41), channel_id=1, source_target_pairs={{0,254},{1,255},{2,0},{3,1},{4,2},{5,3},{6,4},{7,5},{8,6},{9,7},{1... | collective-permute-start | bytes 393224 | tf_op jit(solution)/shard_map/ppermute | solution.py:20
  91.7 10.5 %collective-permute-start.23 = (bf16[1,2,256,128]{3,2,1,0:T(8,128)(2,1)S(1)}, bf16[1,2,256,128]{3,2,1,0:T(8,128)(2,1)S(1)}, u32[]{:S(2)}, u32[]{:S(2)}) collective-permute-start(bf16[1,2,256,128]{3,2,1,0:T(8,128)(2,1)S(1)} %get-tuple-element.42), channel_id=1, source_target_pairs={{0,252},{1,253},{2,254},{3,255},{4,0},{5,1},{6,2},{7,3},{8,4},{9,5... | collective-permute-start | bytes 393224 | tf_op jit(solution)/shard_map/ppermute | solution.py:20
  93.3 12.9 %collective-permute-start.13 = (bf16[128,1,8,128]{3,2,1,0:T(8,128)(2,1)S(1)}, bf16[128,1,8,128]{3,2,1,0:T(8,128)(2,1)S(1)}, u32[]{:S(2)}, u32[]{:S(2)}) collective-permute-start(bf16[128,1,8,128]{3,2,1,0:T(8,128)(2,1)S(1)} %get-tuple-element.28), channel_id=1, source_target_pairs={{0,1},{1,0},{2,3},{3,2},{4,5},{5,4},{6,7},{7,6},{8,9},{9,8},{10,11... | collective-permute-start | bytes 786440 | tf_op jit(solution)/shard_map/ppermute | solution.py:25
  98.6 7.5 %collective-permute-start.12 = (bf16[128,1,8,128]{3,2,1,0:T(8,128)(2,1)S(1)}, bf16[128,1,8,128]{3,2,1,0:T(8,128)(2,1)S(1)}, u32[]{:S(2)}, u32[]{:S(2)}) collective-permute-start(bf16[128,1,8,128]{3,2,1,0:T(8,128)(2,1)S(1)} %get-tuple-element.27), channel_id=1, source_target_pairs={{0,1},{1,0},{2,3},{3,2},{4,5},{5,4},{6,7},{7,6},{8,9},{9,8},{10,11... | collective-permute-start | bytes 786440 | tf_op jit(solution)/shard_map/ppermute | solution.py:25
  98.7 7.6 %collective-permute-start.14 = (bf16[128,1,8,128]{3,2,1,0:T(8,128)(2,1)S(1)}, bf16[128,1,8,128]{3,2,1,0:T(8,128)(2,1)S(1)}, u32[]{:S(2)}, u32[]{:S(2)}) collective-permute-start(bf16[128,1,8,128]{3,2,1,0:T(8,128)(2,1)S(1)} %get-tuple-element.29), channel_id=1, source_target_pairs={{0,1},{1,0},{2,3},{3,2},{4,5},{5,4},{6,7},{7,6},{8,9},{9,8},{10,11... | collective-permute-start | bytes 786440 | tf_op jit(solution)/shard_map/ppermute | solution.py:25
  102.0 4.3 %collective-permute-start.15 = (bf16[128,1,8,128]{3,2,1,0:T(8,128)(2,1)S(1)}, bf16[128,1,8,128]{3,2,1,0:T(8,128)(2,1)S(1)}, u32[]{:S(2)}, u32[]{:S(2)}) collective-permute-start(bf16[128,1,8,128]{3,2,1,0:T(8,128)(2,1)S(1)} %get-tuple-element.30), channel_id=1, source_target_pairs={{0,1},{1,0},{2,3},{3,2},{4,5},{5,4},{6,7},{7,6},{8,9},{9,8},{10,11... | collective-permute-start | bytes 786440 | tf_op jit(solution)/shard_map/ppermute | solution.py:25
  102.3 5.9 %collective-permute-start.24 = (bf16[4,2,128,128]{3,2,1,0:T(8,128)(2,1)S(1)}, bf16[4,2,128,128]{3,2,1,0:T(8,128)(2,1)S(1)}, u32[]{:S(2)}, u32[]{:S(2)}) collective-permute-start(bf16[4,2,128,128]{3,2,1,0:T(8,128)(2,1)S(1)} %dynamic-slice_bitcast_fusion), channel_id=1, source_target_pairs={{0,1},{1,0},{2,3},{3,2},{4,5},{5,4},{6,7},{7,6},{8,9},{9,8},{10,11... | collective-permute-start | bytes 786440 | tf_op jit(solution)/shard_map/ppermute | solution.py:25

commit v2 on v1

v2 whole, which is shorter than its diff:
```python
import functools
import math

import jax
import jax.numpy as jnp
from jax import lax
from jax.experimental import pallas as pl
from jax.experimental.pallas import tpu as pltpu
from jax.sharding import PartitionSpec as P

AXES = ("ctx", "head")
BLK = 128
NEG = -1e30
SCALE = BLK ** (-0.5)
CHUNKS = (2, 2)
VMEM = 28 << 20
DELTA_VMEM = 57 << 20


def chip_shift(x, chips):
    n = lax.axis_size("ctx") * lax.axis_size("head")
    return lax.ppermute(x, AXES, [(i, (i + 2 * chips) % n) for i in range(n)])


def swap_cores(x):
    n = lax.axis_size("ctx") * lax.axis_size("head")
    return lax.ppermute(x, AXES, [(i, i ^ 1) for i in range(n)])


def gather_kernel(slot, scal, k, v, *refs):
    outs, tmp = refs[-len(CHUNKS) - 1 : -1], refs[-1]
    core = scal[0]
    rb = core if slot == 0 else 1 - core
    rows = pl.ds(pl.multiple_of(rb * BLK, BLK), BLK)
    for kind, src in enumerate((k, v)):
        tmp[...] = src[...].astype(jnp.float32).reshape(BLK * 8, BLK)
        h = 0
        for out in outs:
            for i in range(out.shape[0]):
                part = tmp[pl.ds(4 * core + h, BLK, stride=8), :]
                out[i, kind, rows, :] = part.astype(jnp.bfloat16)
                h += 1


def gather_call(core, slot, k, v, chain):
    vm = pl.BlockSpec(memory_space=pltpu.VMEM)
    return pl.pallas_call(
        functools.partial(gather_kernel, slot),
        in_specs=[pl.BlockSpec(memory_space=pltpu.SMEM)] + [vm] * (2 + len(chain)),
        out_specs=[vm] * len(CHUNKS),
        out_shape=[jax.ShapeDtypeStruct((nh, 2, 256, BLK), jnp.bfloat16) for nh in CHUNKS],
        scratch_shapes=[pltpu.VMEM((BLK * 8, BLK), jnp.float32)],
        input_output_aliases={3 + i: i for i in range(len(chain))},
        compiler_params=pltpu.CompilerParams(vmem_limit_bytes=VMEM),
        cost_estimate=pl.CostEstimate(flops=0, bytes_accessed=1 << 19, transcendentals=0),
        name="gather_heads",
    )(core, k, v, *chain)


def final_sum_kernel(scal, *refs):
    n = len(CHUNKS)
    core = scal[0]
    own, a, b = refs[:n], refs[n : 2 * n], refs[2 * n : 3 * n]
    keep, send = refs[3 * n :]
    h = 0
    for c in range(n):
        for i in range(CHUNKS[c]):
            for kind in range(2):
                for out, rb in ((keep, core), (send, 1 - core)):
                    rows = pl.ds(pl.multiple_of(rb * BLK, BLK), BLK)
                    out[h, kind] = (
                        own[c][i, kind, rows, :]
                        + a[c][i, kind, rows, :].astype(jnp.float32)
                        + b[c][i, kind, rows, :].astype(jnp.float32)
                    ).astype(jnp.bfloat16)
            h += 1


def final_sum_call(core, own, a, b):
    vm = pl.BlockSpec(memory_space=pltpu.VMEM)
    shape = jax.ShapeDtypeStruct((4, 2, BLK, BLK), jnp.bfloat16)
    return pl.pallas_call(
        final_sum_kernel,
        in_specs=[pl.BlockSpec(memory_space=pltpu.SMEM)] + [vm] * (3 * len(CHUNKS)),
        out_specs=[vm, vm],
        out_shape=[shape, shape],
        cost_estimate=pl.CostEstimate(flops=0, bytes_accessed=3 << 20, transcendentals=0),
        compiler_params=pltpu.CompilerParams(vmem_limit_bytes=VMEM),
        name="final_sum",
    )(core, *own, *a, *b)


def home_kernel(scal, keep, got, full, *refs):
    n = len(CHUNKS)
    parts, (dk, dv, dq, tmp, sems) = refs[:n], refs[n:]
    core = scal[0]
    copies = []
    h = 4 * (1 - core)
    for c in range(n):
        dst = dq.at[:, pl.ds(h, CHUNKS[c])]
        copies.append(pltpu.make_async_copy(parts[c], dst, sems.at[c]))
        h += CHUNKS[c]
    for copy in copies:
        copy.start()
    for kind, out in enumerate((dk, dv)):
        for src, side in ((keep, core), (got, 1 - core)):
            for i in range(4):
                tmp[pl.ds(4 * side + i, BLK, stride=8), :] = src[i, kind].astype(jnp.float32)
        out[...] = tmp[...].reshape(BLK, 8, BLK).astype(jnp.bfloat16)
    for copy in copies:
        copy.wait()


def home_call(core, keep, got, full, parts):
    vm = pl.BlockSpec(memory_space=pltpu.VMEM)
    hbm = pl.BlockSpec(memory_space=pl.ANY)
    shape = jax.ShapeDtypeStruct((BLK, 8, BLK), jnp.bfloat16)
    return pl.pallas_call(
        home_kernel,
        in_specs=[pl.BlockSpec(memory_space=pltpu.SMEM), vm, vm, hbm] + [hbm] * len(parts),
        out_specs=[vm, vm, hbm],
        out_shape=[shape, shape, jax.ShapeDtypeStruct(full.shape, full.dtype)],
        scratch_shapes=[
            pltpu.VMEM((BLK * 8, BLK), jnp.float32),
            pltpu.SemaphoreType.DMA((len(parts),)),
        ],
        input_output_aliases={3: 2},
        compiler_params=pltpu.CompilerParams(vmem_limit_bytes=VMEM),
        cost_estimate=pl.CostEstimate(flops=0, bytes_accessed=3 << 20, transcendentals=0),
        name="home_heads",
    )(core, keep, got, full, *parts)


def chunk_kernel(
    scal, q_own, q_twin, g_own, g_twin, d_own, d_twin, start, kv_own, kv_a, kv_b,
    dq_own, dq_twin, dkv_own, dkv_a, dkv_b,
    kbuf, vbuf, dk, dv,
):
    core = scal[0]
    rows = BLK * 8
    for n, src in enumerate((kv_b, kv_a, kv_own)):
        kbuf[256 * n : 256 * (n + 1), :] = src[0]
        vbuf[256 * n : 256 * (n + 1), :] = src[1]
    dk[...] = jnp.zeros_like(dk)
    dv[...] = jnp.zeros_like(dv)
    nt = (((1,), (1,)), ((), ()))
    tn = (((0,), (0,)), ((), ()))
    tok = lax.broadcasted_iota(jnp.int32, (1, rows), 1) >> 3
    sides = ((q_own, g_own, d_own, dq_own), (q_twin, g_twin, d_twin, dq_twin))
    for slot, (q, g, d, dq) in enumerate(sides):
        rb = core if slot == 0 else 1 - core
        win = pl.ds(pl.multiple_of(rb * BLK, BLK), 5 * BLK)
        q_t = q[...].astype(jnp.float32).reshape(rows, BLK).astype(jnp.bfloat16)
        g_t = g[...].astype(jnp.float32).reshape(rows, BLK).astype(jnp.bfloat16)
        s = lax.dot_general(kbuf[win, :], q_t, nt, preferred_element_type=jnp.float32)
        u = lax.broadcasted_iota(jnp.int32, s.shape, 0)
        s = jnp.where(u >= start[rb], s, NEG)
        w = lax.broadcasted_iota(jnp.int32, (BLK, rows), 0)
        s = jnp.concatenate([s[: 4 * BLK], jnp.where(w <= tok, s[4 * BLK :], NEG)], axis=0)
        m = jnp.max(s, axis=0, keepdims=True)
        e = jnp.exp2((s - m) * (SCALE * math.log2(math.e)))
        p = e * (1.0 / jnp.sum(e, axis=0, keepdims=True))
        dp = lax.dot_general(vbuf[win, :], g_t, nt, preferred_element_type=jnp.float32)
        dsc = (p * (dp - d[...])).astype(jnp.bfloat16)
        dv[win, :] += jnp.dot(p.astype(jnp.bfloat16), g_t, preferred_element_type=jnp.float32)
        dk[win, :] += jnp.dot(dsc, q_t, preferred_element_type=jnp.float32)
        dqn = lax.dot_general(dsc, kbuf[win, :], tn, preferred_element_type=jnp.float32)
        dq[...] = (dqn * SCALE).reshape(BLK, 8, BLK).astype(jnp.bfloat16)
    for n, dst in enumerate((dkv_b, dkv_a, dkv_own)):
        dst[0] = (dk[256 * n : 256 * (n + 1), :] * SCALE).astype(dst.dtype)
        dst[1] = dv[256 * n : 256 * (n + 1), :].astype(dst.dtype)


def chained_kernel(*refs):
    chunk_kernel(*refs[:11], *refs[12:])


def delta_kernel(o, g, out):
    x = o[...].astype(jnp.float32) * g[...].astype(jnp.float32)
    ones = jnp.ones((8, 2 * BLK), jnp.bfloat16)
    for j in range(8):
        part = x[:, j].reshape(BLK, BLK)
        high = part.astype(jnp.bfloat16)
        low = (part - high.astype(jnp.float32)).astype(jnp.bfloat16)
        r = lax.dot_general(
            ones,
            jnp.concatenate([high, low], axis=1),
            (((1,), (1,)), ((), ())),
            preferred_element_type=jnp.float32,
        )
        out[j] = r[:1]


def delta_call(o4, g4):
    spec = pl.BlockSpec((16, 8, 8, BLK), lambda i: (i, 0, 0, 0))
    return pl.pallas_call(
        delta_kernel,
        grid=(BLK // 16,),
        in_specs=[spec, spec],
        out_specs=pl.BlockSpec((8, 1, BLK), lambda i: (0, 0, i)),
        out_shape=jax.ShapeDtypeStruct((8, 1, BLK * 8), jnp.float32),
        compiler_params=pltpu.CompilerParams(vmem_limit_bytes=DELTA_VMEM),
        cost_estimate=pl.CostEstimate(
            flops=1 << 21, bytes_accessed=4 << 20, transcendentals=0
        ),
        name="delta",
    )(o4, g4)


def chunk_call(
    core, h0, nh, q4, qt, g4, gt, d_own, d_twin, start, kv_own, kv_a, kv_b, dq
):
    rows = BLK * 8
    own = pl.BlockSpec((BLK, None, 8, BLK), lambda h, s: (0, 4 * s[0] + h0 + h, 0, 0))
    d_o = pl.BlockSpec((None, 1, rows), lambda h, s: (4 * s[0] + h0 + h, 0, 0))
    st = pl.BlockSpec((2, 1, rows), lambda h, s: (0, 0, 0))
    kvc = pl.BlockSpec((None, 2, 256, BLK), lambda h, s: (h, 0, 0, 0))
    dqs = pl.BlockSpec((BLK, None, 8, BLK), lambda h, s: (0, h, 0, 0))
    chain = [] if dq is None else [dq]
    return pl.pallas_call(
        chunk_kernel if dq is None else chained_kernel,
        grid_spec=pltpu.PrefetchScalarGridSpec(
            num_scalar_prefetch=1,
            grid=(nh,),
            in_specs=[own, own, own, own, d_o, d_o, st, kvc, kvc, kvc]
            + [pl.BlockSpec(memory_space=pl.ANY)] * len(chain),
            out_specs=[own, dqs, kvc, kvc, kvc],
            scratch_shapes=[
                pltpu.VMEM((768, BLK), jnp.bfloat16),
                pltpu.VMEM((768, BLK), jnp.bfloat16),
                pltpu.VMEM((768, BLK), jnp.float32),
                pltpu.VMEM((768, BLK), jnp.float32),
            ],
        ),
        out_shape=[
            jax.ShapeDtypeStruct((BLK, 8, 8, BLK), jnp.bfloat16),
            jax.ShapeDtypeStruct((BLK, nh, 8, BLK), jnp.bfloat16),
            jax.ShapeDtypeStruct((nh, 2, 256, BLK), jnp.float32),
            jax.ShapeDtypeStruct((nh, 2, 256, BLK), jnp.bfloat16),
            jax.ShapeDtypeStruct((nh, 2, 256, BLK), jnp.bfloat16),
        ],
        compiler_params=pltpu.CompilerParams(vmem_limit_bytes=VMEM),
        input_output_aliases={} if dq is None else {11: 0},
        cost_estimate=pl.CostEstimate(
            flops=nh * 2 * 5 * 2 * rows * 640 * 128,
            bytes_accessed=nh * (6 * rows * 256 + 7 * 131072),
            transcendentals=nh * 2 * rows * 640,
        ),
        name="attention_chunk",
    )(core, q4, qt, g4, gt, d_own, d_twin, start, kv_own, kv_a, kv_b, *chain)


def shards(queries, keys, values, outputs, out_grad, segments):
    dev = lax.axis_index("ctx") * lax.axis_size("head") + lax.axis_index("head")
    core = (dev & 1).reshape(1)
    chip = dev >> 1

    k_twin, v_twin = swap_cores(keys), swap_cores(values)
    seg_pad = jnp.concatenate([jnp.full((512,), -1, jnp.int32), segments])
    seg_w = lax.dynamic_slice_in_dim(seg_pad, chip * 256, 768, 0)
    rows = jnp.broadcast_to(seg_w[512:, None], (256, 8)).reshape(2, 1, BLK * 8)
    first = jnp.sum((seg_w[:, None, None, None] < rows[None]).astype(jnp.int32), axis=0)
    start = first - jnp.array([[[0]], [[BLK]]], jnp.int32)

    half = gather_call(core, 0, keys, values, [])
    k_twin, v_twin, start = lax.optimization_barrier((k_twin, v_twin, start))
    kv_own = gather_call(core, 1, k_twin, v_twin, half)
    queries, out_grad, outputs, *kv_own = lax.optimization_barrier(
        (queries, out_grad, outputs, *kv_own)
    )
    kv_a = [chip_shift(x, 1) for x in kv_own[:2]]
    kv_b = [chip_shift(x, 2) for x in kv_own[:2]]
    q4 = queries.reshape(BLK, 8, 8, BLK)
    g4 = out_grad.reshape(BLK, 8, 8, BLK)
    qt, gt = swap_cores(q4), swap_cores(g4)
    delta = delta_call(outputs.reshape(BLK, 8, 8, BLK), g4)
    d_twin = swap_cores(delta)

    dq, dq_twin, own, back_a, back_b = None, [], [], [], []
    h0 = 0
    for c, nh in enumerate(CHUNKS):
        if c >= 2:
            kv_own[c], own[c - 2] = lax.optimization_barrier((kv_own[c], own[c - 2]))
        if c >= len(kv_a):
            kv_a.append(chip_shift(kv_own[c], 1))
            kv_b.append(chip_shift(kv_own[c], 2))
        dq, t, dkv_o, dkv_a, dkv_b = chunk_call(
            core, h0, nh, q4, qt, g4, gt, delta, d_twin, start, kv_own[c], kv_a[c], kv_b[c], dq
        )
        h0 += nh
        own.append(dkv_o)
        if c:
            dkv_a, dkv_b, back_a[-1], back_b[-1] = lax.optimization_barrier(
                (dkv_a, dkv_b, back_a[-1], back_b[-1])
            )
        back_b.append(chip_shift(dkv_b, -2))
        back_a.append(chip_shift(dkv_a, -1))
        dq_twin.append(swap_cores(t))
    keep, send = final_sum_call(core, own, back_a, back_b)
    dkeys, dvals, dq = home_call(core, keep, swap_cores(send), dq, dq_twin)
    return dq.reshape(BLK, 64, BLK), dkeys, dvals


def solution(mesh):
    spec = P(AXES, None, None)
    return jax.shard_map(
        shards,
        mesh=mesh,
        in_specs=(spec, spec, spec, spec, spec, P()),
        out_specs=(spec, spec, spec),
        check_vma=False,
    )
```

time: 110 us -> 77.5 us (0.70)
  the two profiles are of different devices: /device:TPU:17 before, /device:TPU:127 now
where the time goes in v2:
time: 77.5 us; the launch traced here: 77.1 us
  Pallas kernels  31.1 us (40%)
  starting transfers between devices  22.4 us (29%)
  waiting for transfers between devices  18.2 us (23%)
  local copies, waits for them, and re-layouts  3.65 us (5%)
  between operations  0.91 us (1%)
    pallas_call x2, Pallas kernels, chunk_call(): pl.pallas_call(chunk_kernel if dq is None else chained_kernel, grid_spec=...  22.1 us
    ppermute x8, waiting for transfers between devices, chip_shift(): return lax.ppermute(x, AXES, [(i, (i + 2 * chips) % n) for i in range(n)])  16 us
    ppermute x8, starting transfers between devices, chip_shift(): return lax.ppermute(x, AXES, [(i, (i + 2 * chips) % n) for i in range(n)])  13.3 us
    ppermute x8, starting transfers between devices, swap_cores(): return lax.ppermute(x, AXES, [(i, i ^ 1) for i in range(n)])  9.14 us
    pallas_call x1, Pallas kernels, delta_call(): pl.pallas_call(delta_kernel, grid=(BLK // 16,), in_specs=[spec, spec], ou...  6.7 us
    unnamed x12, local copies, waits for them, and re-layouts  2.66 us
    ppermute x8, waiting for transfers between devices, swap_cores(): return lax.ppermute(x, AXES, [(i, i ^ 1) for i in range(n)])  2.24 us
    pallas_call x1, Pallas kernels, home_call(): pl.pallas_call(home_kernel, in_specs=[pl.BlockSpec(memory_space=pltpu.SME...  1.77 us
  transfers between devices with their start and end apart: 16, of which 6 were waited for; matrix products, arithmetic and copies ran while one was open for 2% of the time, Pallas kernels for 38%

profile of v2, /device:TPU:127, one launch (start us, length us, event | category | flops | bytes accessed | tf_op | source)
XLA Modules:
  0.0 77.1 jit_solution(3679173430489062021)
XLA Ops:
  0.6 0.8 collective-permute-start
  1.4 0.1 collective-permute-start.1
  1.5 0.8 %pad_dynamic-slice_fusion = s32[768]{0:T(1024)S(1)} fusion(s32[]{:T(128)S(6)} %select_n.3, s32[32768]{0:T(1024)} %param.12), kind=kLoop, calls=%fused_computation.1 | loop fusion | bytes 134148 | tf_op jit(solution)/shard_map/dynamic_slice | solution.py:260
  2.4 0.1 broadcast_in_dim.5
  2.5 0.7 convert_reduce_fusion
  3.2 0.9 %copy-done.1 = bf16[128,8,128]{2,1,0:T(8,128)(2,1)S(1)} copy-done((bf16[128,8,128]{2,1,0:T(8,128)(2,1)S(1)}, bf16[128,8,128]{2,1,0:T(8,128)(2,1)}, u32[]{:S(2)}) %copy-start.1) | copy-done | bytes 262168
  4.2 0.9 %copy-done.2 = bf16[128,8,128]{2,1,0:T(8,128)(2,1)S(1)} copy-done((bf16[128,8,128]{2,1,0:T(8,128)(2,1)S(1)}, bf16[128,8,128]{2,1,0:T(8,128)(2,1)}, u32[]{:S(2)}) %copy-start.2) | copy-done | bytes 262168
  5.1 0.2 gather_heads.2
  5.4 0.2 gather_heads.3
  5.6 0.5 collective-permute-start.2
  6.1 0.1 collective-permute-start.3
  6.2 3.4 %collective-permute-start.6 = (bf16[2,2,256,128]{3,2,1,0:T(8,128)(2,1)S(1)}, bf16[2,2,256,128]{3,2,1,0:T(8,128)(2,1)S(1)}, u32[]{:S(2)}, u32[]{:S(2)}) collective-permute-start(bf16[2,2,256,128]{3,2,1,0:T(8,128)(2,1)S(1)} %get-tuple-element.44.kv_own), channel_id=1, source_target_pairs={{0,4},{1,5},{2,6},{3,7},{4,8},{5,9},{6,10},{7,11},{8,12},{9,13},{1... | collective-permute-start | bytes 786440 | tf_op jit(solution)/shard_map/ppermute | solution.py:22
  9.6 1.9 %collective-permute-start.5 = (bf16[2,2,256,128]{3,2,1,0:T(8,128)(2,1)S(1)}, bf16[2,2,256,128]{3,2,1,0:T(8,128)(2,1)}, u32[]{:S(2)}, u32[]{:S(2)}) collective-permute-start(bf16[2,2,256,128]{3,2,1,0:T(8,128)(2,1)S(1)} %get-tuple-element.44.kv_own), channel_id=1, source_target_pairs={{0,2},{1,3},{2,4},{3,5},{4,6},{5,7},{6,8},{7,9},{8,10},{9,11},{10,... | collective-permute-start | bytes 786440 | tf_op jit(solution)/shard_map/ppermute | solution.py:22
  11.5 6.7 %delta.1.d_own.refs_5_ = f32[8,1,1024]{2,1,0:T(1,128)} custom-call(bf16[128,8,8,128]{3,2,1,0:T(8,128)(2,1)} %bitcast.14, bf16[128,8,8,128]{3,2,1,0:T(8,128)(2,1)} %bitcast.8), custom_call_target="tpu_custom_call" | custom-call | flops 2097152 | bytes 4194304 | tf_op jit(solution)/shard_map/delta/pallas_call | solution.py:196
  18.2 1.0 %collective-permute-start.4 = (f32[8,1,1024]{2,1,0:T(1,128)}, f32[8,1,1024]{2,1,0:T(1,128)S(1)}, u32[]{:S(2)}, u32[]{:S(2)}) collective-permute-start(f32[8,1,1024]{2,1,0:T(1,128)} %delta.1.d_own.refs_5_), channel_id=1, source_target_pairs={{0,1},{1,0},{2,3},{3,2},{4,5},{5,4},{6,7},{7,6},{8,9},{9,8},{10,11... | collective-permute-start | bytes 98312 | tf_op jit(solution)/shard_map/ppermute | solution.py:27
  19.2 1.1 %collective-permute-done.4.d_twin.refs_6_ = f32[8,1,1024]{2,1,0:T(1,128)S(1)} collective-permute-done((f32[8,1,1024]{2,1,0:T(1,128)}, f32[8,1,1024]{2,1,0:T(1,128)S(1)}, u32[]{:S(2)}, u32[]{:S(2)}) %collective-permute-start.4) | collective-permute-done | bytes 32800 | tf_op jit(solution)/shard_map/ppermute | solution.py:27
  20.2 1.9 %collective-permute-start.8 = (bf16[2,2,256,128]{3,2,1,0:T(8,128)(2,1)S(1)}, bf16[2,2,256,128]{3,2,1,0:T(8,128)(2,1)S(1)}, u32[]{:S(2)}, u32[]{:S(2)}) collective-permute-start(bf16[2,2,256,128]{3,2,1,0:T(8,128)(2,1)S(1)} %get-tuple-element.46.refs_8_), channel_id=1, source_target_pairs={{0,4},{1,5},{2,6},{3,7},{4,8},{5,9},{6,10},{7,11},{8,12},{9,13},{1... | collective-permute-start | bytes 786440 | tf_op jit(solution)/shard_map/ppermute | solution.py:22
  22.2 2.5 %collective-permute-start.7 = (bf16[2,2,256,128]{3,2,1,0:T(8,128)(2,1)S(1)}, bf16[2,2,256,128]{3,2,1,0:T(8,128)(2,1)S(1)}, u32[]{:S(2)}, u32[]{:S(2)}) collective-permute-start(bf16[2,2,256,128]{3,2,1,0:T(8,128)(2,1)S(1)} %get-tuple-element.46.refs_8_), channel_id=1, source_target_pairs={{0,2},{1,3},{2,4},{3,5},{4,6},{5,7},{6,8},{7,9},{8,10},{9,11},{10,... | collective-permute-start | bytes 786440 | tf_op jit(solution)/shard_map/ppermute | solution.py:22
  24.7 0.7 copy-done.3
  25.5 11.1 %attention_chunk.2 = (bf16[128,8,8,128]{3,2,1,0:T(8,128)(2,1)}, bf16[128,2,8,128]{3,2,1,0:T(8,128)(2,1)S(1)}, f32[2,2,256,128]{3,2,1,0:T(8,128)S(1)}, bf16[2,2,2...) custom-call(s32[1]{0:T(128)} %bitcast.scal.refs_0_, bf16[128,8,8,128]{3,2,1,0:T(8,128)(2,1)S(1)} %bitcast.12, ...), custom_call_target="tpu_custom_call" | custom-call | flops 3355443200 | bytes 4980736 | tf_op jit(solution)/shard_map/attention_chunk/pallas_call | solution.py:220
  36.5 0.4 collective-permute-start.10
  37.0 11.1 %attention_chunk.3 = (bf16[128,8,8,128]{3,2,1,0:T(8,128)(2,1)}, bf16[128,2,8,128]{3,2,1,0:T(8,128)(2,1)S(1)}, f32[2,2,256,128]{3,2,1,0:T(8,128)S(1)}, bf16[2,2,2...) custom-call(s32[1]{0:T(128)} %bitcast.scal.refs_0_, ...), custom_call_target="tpu_custom_call", output_to_operand_aliasing={{0}: (11, {})} | custom-call | flops 3355443200 | bytes 4980736 | tf_op jit(solution)/shard_map/attention_chunk/pallas_call | solution.py:220
  48.0 3.8 %collective-permute-done.9.refs_2_ = bf16[2,2,256,128]{3,2,1,0:T(8,128)(2,1)S(1)} collective-permute-done((bf16[2,2,256,128]{3,2,1,0:T(8,128)(2,1)S(1)}, bf16[2,2,256,128]{3,2,1,0:T(8,128)(2,1)S(1)}, u32[]{:S(2)}, u32[]{:S(2)}) %collective-permute-start.9) | collective-permute-done | bytes 262176 | tf_op jit(solution)/shard_map/ppermute | solution.py:22
  51.9 1.5 %collective-permute-done.10.refs_4_ = bf16[2,2,256,128]{3,2,1,0:T(8,128)(2,1)S(1)} collective-permute-done((bf16[2,2,256,128]{3,2,1,0:T(8,128)(2,1)S(1)}, bf16[2,2,256,128]{3,2,1,0:T(8,128)(2,1)S(1)}, u32[]{:S(2)}, u32[]{:S(2)}) %collective-permute-start.10) | collective-permute-done | bytes 262176 | tf_op jit(solution)/shard_map/ppermute | solution.py:22
  53.4 3.1 %collective-permute-start.11 = (bf16[2,2,256,128]{3,2,1,0:T(8,128)(2,1)S(1)}, bf16[2,2,256,128]{3,2,1,0:T(8,128)(2,1)S(1)}, u32[]{:S(2)}, u32[]{:S(2)}) collective-permute-start(bf16[2,2,256,128]{3,2,1,0:T(8,128)(2,1)S(1)} %get-tuple-element.54), channel_id=1, source_target_pairs={{0,254},{1,255},{2,0},{3,1},{4,2},{5,3},{6,4},{7,5},{8,6},{9,7},{1... | collective-permute-start | bytes 786440 | tf_op jit(solution)/shard_map/ppermute | solution.py:22
  56.5 2.1 %collective-permute-start.15 = (bf16[128,2,8,128]{3,2,1,0:T(8,128)(2,1)S(1)}, bf16[128,2,8,128]{3,2,1,0:T(8,128)(2,1)S(1)}, u32[]{:S(2)}, u32[]{:S(2)}) collective-permute-start(bf16[128,2,8,128]{3,2,1,0:T(8,128)(2,1)S(1)} %get-tuple-element.61), channel_id=1, source_target_pairs={{0,1},{1,0},{2,3},{3,2},{4,5},{5,4},{6,7},{7,6},{8,9},{9,8},{10,11... | collective-permute-start | bytes 1572872 | tf_op jit(solution)/shard_map/ppermute | solution.py:27
  58.6 5.4 %collective-permute-done.11.refs_3_ = bf16[2,2,256,128]{3,2,1,0:T(8,128)(2,1)S(1)} collective-permute-done((bf16[2,2,256,128]{3,2,1,0:T(8,128)(2,1)S(1)}, bf16[2,2,256,128]{3,2,1,0:T(8,128)(2,1)S(1)}, u32[]{:S(2)}, u32[]{:S(2)}) %collective-permute-start.11) | collective-permute-done | bytes 262176 | tf_op jit(solution)/shard_map/ppermute | solution.py:22
  64.0 5.2 %collective-permute-done.12.refs_5_ = bf16[2,2,256,128]{3,2,1,0:T(8,128)(2,1)S(1)} collective-permute-done((bf16[2,2,256,128]{3,2,1,0:T(8,128)(2,1)S(1)}, bf16[2,2,256,128]{3,2,1,0:T(8,128)(2,1)S(1)}, u32[]{:S(2)}, u32[]{:S(2)}) %collective-permute-start.12) | collective-permute-done | bytes 262176 | tf_op jit(solution)/shard_map/ppermute | solution.py:22
  69.2 0.2 final_sum.1
  69.4 4.6 %collective-permute-start.13 = (bf16[4,2,128,128]{3,2,1,0:T(8,128)(2,1)S(1)}, bf16[4,2,128,128]{3,2,1,0:T(8,128)(2,1)S(1)}, u32[]{:S(2)}, u32[]{:S(2)}) collective-permute-start(bf16[4,2,128,128]{3,2,1,0:T(8,128)(2,1)S(1)} %get-tuple-element.58), channel_id=1, source_target_pairs={{0,1},{1,0},{2,3},{3,2},{4,5},{5,4},{6,7},{7,6},{8,9},{9,8},{10,11... | collective-permute-start | bytes 786440 | tf_op jit(solution)/shard_map/ppermute | solution.py:27
  74.0 1.2 %collective-permute-done.13.got = bf16[4,2,128,128]{3,2,1,0:T(8,128)(2,1)S(1)} collective-permute-done((bf16[4,2,128,128]{3,2,1,0:T(8,128)(2,1)S(1)}, bf16[4,2,128,128]{3,2,1,0:T(8,128)(2,1)S(1)}, u32[]{:S(2)}, u32[]{:S(2)}) %collective-permute-start.13) | collective-permute-done | bytes 262176 | tf_op jit(solution)/shard_map/ppermute | solution.py:27
  75.1 1.8 %home_heads.1 = (bf16[128,8,128]{2,1,0:T(8,128)(2,1)}, bf16[128,8,128]{2,1,0:T(8,128)(2,1)}, bf16[128,8,8,128]{3,2,1,0:T(8,128)(2,1)}) custom-call(s32[1]{0:T(128)} %bitcast.scal.refs_0_, bf16[4,2,128,128]{3,2,1,0:T(8,128)(2,1)S(1)} %get-tuple-element.57.keep, ...), custom_call_target="tpu_custom_call", output_to_operand_aliasing={{2}: (3, {})} | custom-call | bytes 3145728 | tf_op jit(solution)/shard_map/home_heads/pallas_call | solution.py:118
  (26 shorter events, 0.2 us)
Async XLA Ops:
  0.6 4.7 %collective-permute-start = (bf16[128,8,128]{2,1,0:T(8,128)(2,1)}, bf16[128,8,128]{2,1,0:T(8,128)(2,1)S(1)}, u32[]{:S(2)}, u32[]{:S(2)}) collective-permute-start(bf16[128,8,128]{2,1,0:T(8,128)(2,1)} %k.1), channel_id=1, source_target_pairs={{0,1},{1,0},{2,3},{3,2},{4,5},{5,4},{6,7},{7,6},{8,9},{9,8},{10,11... | collective-permute-start | bytes 786440 | tf_op jit(solution)/shard_map/ppermute | solution.py:27
  1.4 4.0 %collective-permute-start.1 = (bf16[128,8,128]{2,1,0:T(8,128)(2,1)}, bf16[128,8,128]{2,1,0:T(8,128)(2,1)S(1)}, u32[]{:S(2)}, u32[]{:S(2)}) collective-permute-start(bf16[128,8,128]{2,1,0:T(8,128)(2,1)} %v.1), channel_id=1, source_target_pairs={{0,1},{1,0},{2,3},{3,2},{4,5},{5,4},{6,7},{7,6},{8,9},{9,8},{10,11... | collective-permute-start | bytes 786440 | tf_op jit(solution)/shard_map/ppermute | solution.py:27
  3.2 1.0 %copy-start.1 = (bf16[128,8,128]{2,1,0:T(8,128)(2,1)S(1)}, bf16[128,8,128]{2,1,0:T(8,128)(2,1)}, u32[]{:S(2)}) copy-start(bf16[128,8,128]{2,1,0:T(8,128)(2,1)} %k.1) | copy-start | bytes 786436
  4.2 0.9 %copy-start.2 = (bf16[128,8,128]{2,1,0:T(8,128)(2,1)S(1)}, bf16[128,8,128]{2,1,0:T(8,128)(2,1)}, u32[]{:S(2)}) copy-start(bf16[128,8,128]{2,1,0:T(8,128)(2,1)} %v.1) | copy-start | bytes 786436
  5.6 19.1 %collective-permute-start.2 = (bf16[128,8,8,128]{3,2,1,0:T(8,128)(2,1)}, bf16[128,8,8,128]{3,2,1,0:T(8,128)(2,1)S(1)}, u32[]{:S(2)}, u32[]{:S(2)}) collective-permute-start(bf16[128,8,8,128]{3,2,1,0:T(8,128)(2,1)} %bitcast.11), channel_id=1, source_target_pairs={{0,1},{1,0},{2,3},{3,2},{4,5},{5,4},{6,7},{7,6},{8,9},{9,8},{10,11... | collective-permute-start | bytes 6291464 | tf_op jit(solution)/shard_map/ppermute | solution.py:27
  6.1 18.6 %collective-permute-start.3 = (bf16[128,8,8,128]{3,2,1,0:T(8,128)(2,1)}, bf16[128,8,8,128]{3,2,1,0:T(8,128)(2,1)}, u32[]{:S(2)}, u32[]{:S(2)}) collective-permute-start(bf16[128,8,8,128]{3,2,1,0:T(8,128)(2,1)} %bitcast.7), channel_id=1, source_target_pairs={{0,1},{1,0},{2,3},{3,2},{4,5},{5,4},{6,7},{7,6},{8,9},{9,8},{10,11... | collective-permute-start | bytes 6291464 | tf_op jit(solution)/shard_map/ppermute | solution.py:27
  6.2 16.0 %collective-permute-start.6 = (bf16[2,2,256,128]{3,2,1,0:T(8,128)(2,1)S(1)}, bf16[2,2,256,128]{3,2,1,0:T(8,128)(2,1)S(1)}, u32[]{:S(2)}, u32[]{:S(2)}) collective-permute-start(bf16[2,2,256,128]{3,2,1,0:T(8,128)(2,1)S(1)} %get-tuple-element.44.kv_own), channel_id=1, source_target_pairs={{0,4},{1,5},{2,6},{3,7},{4,8},{5,9},{6,10},{7,11},{8,12},{9,13},{1... | collective-permute-start | bytes 786440 | tf_op jit(solution)/shard_map/ppermute | solution.py:22
  9.6 15.1 %collective-permute-start.5 = (bf16[2,2,256,128]{3,2,1,0:T(8,128)(2,1)S(1)}, bf16[2,2,256,128]{3,2,1,0:T(8,128)(2,1)}, u32[]{:S(2)}, u32[]{:S(2)}) collective-permute-start(bf16[2,2,256,128]{3,2,1,0:T(8,128)(2,1)S(1)} %get-tuple-element.44.kv_own), channel_id=1, source_target_pairs={{0,2},{1,3},{2,4},{3,5},{4,6},{5,7},{6,8},{7,9},{8,10},{9,11},{10,... | collective-permute-start | bytes 786440 | tf_op jit(solution)/shard_map/ppermute | solution.py:22
  11.5 13.2 %copy-start = (bf16[128,64,128]{2,1,0:T(8,128)(2,1)S(1)}, bf16[128,64,128]{2,1,0:T(8,128)(2,1)}, u32[]{:S(2)}) copy-start(bf16[128,64,128]{2,1,0:T(8,128)(2,1)} %param.11) | copy-start | bytes 6291460
  11.5 13.2 %copy-start.5 = (bf16[128,64,128]{2,1,0:T(8,128)(2,1)S(1)}, bf16[128,64,128]{2,1,0:T(8,128)(2,1)}, u32[]{:S(2)}) copy-start(bf16[128,64,128]{2,1,0:T(8,128)(2,1)} %param.7) | copy-start | bytes 6291460
  18.2 2.0 %collective-permute-start.4 = (f32[8,1,1024]{2,1,0:T(1,128)}, f32[8,1,1024]{2,1,0:T(1,128)S(1)}, u32[]{:S(2)}, u32[]{:S(2)}) collective-permute-start(f32[8,1,1024]{2,1,0:T(1,128)} %delta.1.d_own.refs_5_), channel_id=1, source_target_pairs={{0,1},{1,0},{2,3},{3,2},{4,5},{5,4},{6,7},{7,6},{8,9},{9,8},{10,11... | collective-permute-start | bytes 98312 | tf_op jit(solution)/shard_map/ppermute | solution.py:27
  20.2 16.7 %collective-permute-start.8 = (bf16[2,2,256,128]{3,2,1,0:T(8,128)(2,1)S(1)}, bf16[2,2,256,128]{3,2,1,0:T(8,128)(2,1)S(1)}, u32[]{:S(2)}, u32[]{:S(2)}) collective-permute-start(bf16[2,2,256,128]{3,2,1,0:T(8,128)(2,1)S(1)} %get-tuple-element.46.refs_8_), channel_id=1, source_target_pairs={{0,4},{1,5},{2,6},{3,7},{4,8},{5,9},{6,10},{7,11},{8,12},{9,13},{1... | collective-permute-start | bytes 786440 | tf_op jit(solution)/shard_map/ppermute | solution.py:22
  22.2 14.8 %collective-permute-start.7 = (bf16[2,2,256,128]{3,2,1,0:T(8,128)(2,1)S(1)}, bf16[2,2,256,128]{3,2,1,0:T(8,128)(2,1)S(1)}, u32[]{:S(2)}, u32[]{:S(2)}) collective-permute-start(bf16[2,2,256,128]{3,2,1,0:T(8,128)(2,1)S(1)} %get-tuple-element.46.refs_8_), channel_id=1, source_target_pairs={{0,2},{1,3},{2,4},{3,5},{4,6},{5,7},{6,8},{7,9},{8,10},{9,11},{10,... | collective-permute-start | bytes 786440 | tf_op jit(solution)/shard_map/ppermute | solution.py:22
  24.7 0.8 copy-start.3
  25.5 11.5 %copy-start.4 = (f32[8,1,1024]{2,1,0:T(1,128)S(1)}, f32[8,1,1024]{2,1,0:T(1,128)}, u32[]{:S(2)}) copy-start(f32[8,1,1024]{2,1,0:T(1,128)} %delta.1.d_own.refs_5_) | copy-start | bytes 98308
  36.5 15.3 %collective-permute-start.9 = (bf16[2,2,256,128]{3,2,1,0:T(8,128)(2,1)S(1)}, bf16[2,2,256,128]{3,2,1,0:T(8,128)(2,1)S(1)}, u32[]{:S(2)}, u32[]{:S(2)}) collective-permute-start(bf16[2,2,256,128]{3,2,1,0:T(8,128)(2,1)S(1)} %get-tuple-element.51), channel_id=1, source_target_pairs={{0,254},{1,255},{2,0},{3,1},{4,2},{5,3},{6,4},{7,5},{8,6},{9,7},{1... | collective-permute-start | bytes 786440 | tf_op jit(solution)/shard_map/ppermute | solution.py:22
  36.5 16.8 %collective-permute-start.10 = (bf16[2,2,256,128]{3,2,1,0:T(8,128)(2,1)S(1)}, bf16[2,2,256,128]{3,2,1,0:T(8,128)(2,1)S(1)}, u32[]{:S(2)}, u32[]{:S(2)}) collective-permute-start(bf16[2,2,256,128]{3,2,1,0:T(8,128)(2,1)S(1)} %get-tuple-element.52), channel_id=1, source_target_pairs={{0,252},{1,253},{2,254},{3,255},{4,0},{5,1},{6,2},{7,3},{8,4},{9,5... | collective-permute-start | bytes 786440 | tf_op jit(solution)/shard_map/ppermute | solution.py:22
  53.4 10.7 %collective-permute-start.11 = (bf16[2,2,256,128]{3,2,1,0:T(8,128)(2,1)S(1)}, bf16[2,2,256,128]{3,2,1,0:T(8,128)(2,1)S(1)}, u32[]{:S(2)}, u32[]{:S(2)}) collective-permute-start(bf16[2,2,256,128]{3,2,1,0:T(8,128)(2,1)S(1)} %get-tuple-element.54), channel_id=1, source_target_pairs={{0,254},{1,255},{2,0},{3,1},{4,2},{5,3},{6,4},{7,5},{8,6},{9,7},{1... | collective-permute-start | bytes 786440 | tf_op jit(solution)/shard_map/ppermute | solution.py:22
  56.5 12.8 %collective-permute-start.12 = (bf16[2,2,256,128]{3,2,1,0:T(8,128)(2,1)S(1)}, bf16[2,2,256,128]{3,2,1,0:T(8,128)(2,1)S(1)}, u32[]{:S(2)}, u32[]{:S(2)}) collective-permute-start(bf16[2,2,256,128]{3,2,1,0:T(8,128)(2,1)S(1)} %get-tuple-element.56), channel_id=1, source_target_pairs={{0,252},{1,253},{2,254},{3,255},{4,0},{5,1},{6,2},{7,3},{8,4},{9,5... | collective-permute-start | bytes 786440 | tf_op jit(solution)/shard_map/ppermute | solution.py:22
  56.5 17.5 %collective-permute-start.15 = (bf16[128,2,8,128]{3,2,1,0:T(8,128)(2,1)S(1)}, bf16[128,2,8,128]{3,2,1,0:T(8,128)(2,1)S(1)}, u32[]{:S(2)}, u32[]{:S(2)}) collective-permute-start(bf16[128,2,8,128]{3,2,1,0:T(8,128)(2,1)S(1)} %get-tuple-element.61), channel_id=1, source_target_pairs={{0,1},{1,0},{2,3},{3,2},{4,5},{5,4},{6,7},{7,6},{8,9},{9,8},{10,11... | collective-permute-start | bytes 1572872 | tf_op jit(solution)/shard_map/ppermute | solution.py:27
  58.6 15.4 %collective-permute-start.14 = (bf16[128,2,8,128]{3,2,1,0:T(8,128)(2,1)S(1)}, bf16[128,2,8,128]{3,2,1,0:T(8,128)(2,1)S(1)}, u32[]{:S(2)}, u32[]{:S(2)}) collective-permute-start(bf16[128,2,8,128]{3,2,1,0:T(8,128)(2,1)S(1)} %get-tuple-element.60), channel_id=1, source_target_pairs={{0,1},{1,0},{2,3},{3,2},{4,5},{5,4},{6,7},{7,6},{8,9},{9,8},{10,11... | collective-permute-start | bytes 1572872 | tf_op jit(solution)/shard_map/ppermute | solution.py:27
  69.4 5.7 %collective-permute-start.13 = (bf16[4,2,128,128]{3,2,1,0:T(8,128)(2,1)S(1)}, bf16[4,2,128,128]{3,2,1,0:T(8,128)(2,1)S(1)}, u32[]{:S(2)}, u32[]{:S(2)}) collective-permute-start(bf16[4,2,128,128]{3,2,1,0:T(8,128)(2,1)S(1)} %get-tuple-element.58), channel_id=1, source_target_pairs={{0,1},{1,0},{2,3},{3,2},{4,5},{5,4},{6,7},{7,6},{8,9},{9,8},{10,11... | collective-permute-start | bytes 786440 | tf_op jit(solution)/shard_map/ppermute | solution.py:27

commit v3 on v2

--- a/solution.py
+++ b/solution.py
@@ -290,13 +290,13 @@
         h0 += nh
         own.append(dkv_o)
         if c:
-            dkv_a, dkv_b, back_a[-1], back_b[-1] = lax.optimization_barrier(
-                (dkv_a, dkv_b, back_a[-1], back_b[-1])
+            dkv_b, dkv_a, back_b[-1], back_a[-1] = lax.optimization_barrier(
+                (dkv_b, dkv_a, back_b[-1], back_a[-1])
             )
+        back_a.append(chip_shift(dkv_a, -1))
         back_b.append(chip_shift(dkv_b, -2))
-        back_a.append(chip_shift(dkv_a, -1))
         dq_twin.append(swap_cores(t))
-    keep, send = final_sum_call(core, own, back_a, back_b)
+    keep, send = final_sum_call(core, own, back_b, back_a)
     dkeys, dvals, dq = home_call(core, keep, swap_cores(send), dq, dq_twin)
     return dq.reshape(BLK, 64, BLK), dkeys, dvals
 

time: 77.5 us -> 78.3 us (1.010)
  waiting for transfers between devices: 18.2 us -> 23.7 us
  starting transfers between devices: 22.4 us -> 17.8 us
    ppermute x8, waiting for transfers between devices: 16 us -> 21.4 us  [chip_shift(): return lax.ppermute(x, AXES, [(i, (i + 2 * chips) % n) for i in range(n)])]
    ppermute x8, starting transfers between devices: 13.3 us -> 9.77 us  [chip_shift(): return lax.ppermute(x, AXES, [(i, (i + 2 * chips) % n) for i in range(n)])]
    ppermute x8, starting transfers between devices: 9.14 us -> 8 us  [swap_cores(): return lax.ppermute(x, AXES, [(i, i ^ 1) for i in range(n)])]
  transfers between devices with their start and end apart: 16 -> 16, of which waited for: 6 -> 6; matrix products, arithmetic and copies ran while one was open for 2% -> 2% of each run, Pallas kernels for 38% -> 37%
where the time goes in v3:
time: 78.3 us; the launch traced here: 77.9 us
  Pallas kernels  31.1 us (40%)
  waiting for transfers between devices  23.7 us (30%)
  starting transfers between devices  17.8 us (23%)
  local copies, waits for them, and re-layouts  3.65 us (5%)
  between operations  0.93 us (1%)
    pallas_call x2, Pallas kernels, chunk_call(): pl.pallas_call(chunk_kernel if dq is None else chained_kernel, grid_spec=...  22.1 us
    ppermute x8, waiting for transfers between devices, chip_shift(): return lax.ppermute(x, AXES, [(i, (i + 2 * chips) % n) for i in range(n)])  21.4 us
    ppermute x8, starting transfers between devices, chip_shift(): return lax.ppermute(x, AXES, [(i, (i + 2 * chips) % n) for i in range(n)])  9.77 us
    ppermute x8, starting transfers between devices, swap_cores(): return lax.ppermute(x, AXES, [(i, i ^ 1) for i in range(n)])  8 us
    pallas_call x1, Pallas kernels, delta_call(): pl.pallas_call(delta_kernel, grid=(BLK // 16,), in_specs=[spec, spec], ou...  6.7 us
    unnamed x12, local copies, waits for them, and re-layouts  2.66 us
    ppermute x8, waiting for transfers between devices, swap_cores(): return lax.ppermute(x, AXES, [(i, i ^ 1) for i in range(n)])  2.24 us
    pallas_call x1, Pallas kernels, home_call(): pl.pallas_call(home_kernel, in_specs=[pl.BlockSpec(memory_space=pltpu.SME...  1.77 us
  transfers between devices with their start and end apart: 16, of which 6 were waited for; matrix products, arithmetic and copies ran while one was open for 2% of the time, Pallas kernels for 37%

profile of v3, /device:TPU:127, one launch (start us, length us, event | category | flops | bytes accessed | tf_op | source)
XLA Modules:
  0.0 77.9 jit_solution(12769537153092358235)
XLA Ops:
  0.6 0.8 collective-permute-start
  1.4 0.1 collective-permute-start.1
  1.5 0.8 %pad_dynamic-slice_fusion = s32[768]{0:T(1024)S(1)} fusion(s32[]{:T(128)S(6)} %select_n.3, s32[32768]{0:T(1024)} %param.12), kind=kLoop, calls=%fused_computation.1 | loop fusion | bytes 134148 | tf_op jit(solution)/shard_map/dynamic_slice | solution.py:260
  2.3 0.1 broadcast_in_dim.4
  2.4 0.1 broadcast_in_dim.5
  2.5 0.7 convert_reduce_fusion
  3.2 0.9 %copy-done.1 = bf16[128,8,128]{2,1,0:T(8,128)(2,1)S(1)} copy-done((bf16[128,8,128]{2,1,0:T(8,128)(2,1)S(1)}, bf16[128,8,128]{2,1,0:T(8,128)(2,1)}, u32[]{:S(2)}) %copy-start.1) | copy-done | bytes 262168
  4.2 0.9 %copy-done.2 = bf16[128,8,128]{2,1,0:T(8,128)(2,1)S(1)} copy-done((bf16[128,8,128]{2,1,0:T(8,128)(2,1)S(1)}, bf16[128,8,128]{2,1,0:T(8,128)(2,1)}, u32[]{:S(2)}) %copy-start.2) | copy-done | bytes 262168
  5.1 0.2 gather_heads.2
  5.4 0.2 gather_heads.3
  5.6 0.5 collective-permute-start.2
  6.1 0.1 collective-permute-start.3
  6.2 3.4 %collective-permute-start.6 = (bf16[2,2,256,128]{3,2,1,0:T(8,128)(2,1)S(1)}, bf16[2,2,256,128]{3,2,1,0:T(8,128)(2,1)S(1)}, u32[]{:S(2)}, u32[]{:S(2)}) collective-permute-start(bf16[2,2,256,128]{3,2,1,0:T(8,128)(2,1)S(1)} %get-tuple-element.44.kv_own), channel_id=1, source_target_pairs={{0,4},{1,5},{2,6},{3,7},{4,8},{5,9},{6,10},{7,11},{8,12},{9,13},{1... | collective-permute-start | bytes 786440 | tf_op jit(solution)/shard_map/ppermute | solution.py:22
  9.6 1.9 %collective-permute-start.5 = (bf16[2,2,256,128]{3,2,1,0:T(8,128)(2,1)S(1)}, bf16[2,2,256,128]{3,2,1,0:T(8,128)(2,1)}, u32[]{:S(2)}, u32[]{:S(2)}) collective-permute-start(bf16[2,2,256,128]{3,2,1,0:T(8,128)(2,1)S(1)} %get-tuple-element.44.kv_own), channel_id=1, source_target_pairs={{0,2},{1,3},{2,4},{3,5},{4,6},{5,7},{6,8},{7,9},{8,10},{9,11},{10,... | collective-permute-start | bytes 786440 | tf_op jit(solution)/shard_map/ppermute | solution.py:22
  11.5 6.7 %delta.1.d_own.refs_5_ = f32[8,1,1024]{2,1,0:T(1,128)} custom-call(bf16[128,8,8,128]{3,2,1,0:T(8,128)(2,1)} %bitcast.14, bf16[128,8,8,128]{3,2,1,0:T(8,128)(2,1)} %bitcast.8), custom_call_target="tpu_custom_call" | custom-call | flops 2097152 | bytes 4194304 | tf_op jit(solution)/shard_map/delta/pallas_call | solution.py:196
  18.2 1.0 %collective-permute-start.4 = (f32[8,1,1024]{2,1,0:T(1,128)}, f32[8,1,1024]{2,1,0:T(1,128)S(1)}, u32[]{:S(2)}, u32[]{:S(2)}) collective-permute-start(f32[8,1,1024]{2,1,0:T(1,128)} %delta.1.d_own.refs_5_), channel_id=1, source_target_pairs={{0,1},{1,0},{2,3},{3,2},{4,5},{5,4},{6,7},{7,6},{8,9},{9,8},{10,11... | collective-permute-start | bytes 98312 | tf_op jit(solution)/shard_map/ppermute | solution.py:27
  19.2 1.1 %collective-permute-done.4.d_twin.refs_6_ = f32[8,1,1024]{2,1,0:T(1,128)S(1)} collective-permute-done((f32[8,1,1024]{2,1,0:T(1,128)}, f32[8,1,1024]{2,1,0:T(1,128)S(1)}, u32[]{:S(2)}, u32[]{:S(2)}) %collective-permute-start.4) | collective-permute-done | bytes 32800 | tf_op jit(solution)/shard_map/ppermute | solution.py:27
  20.2 1.9 %collective-permute-start.8 = (bf16[2,2,256,128]{3,2,1,0:T(8,128)(2,1)S(1)}, bf16[2,2,256,128]{3,2,1,0:T(8,128)(2,1)S(1)}, u32[]{:S(2)}, u32[]{:S(2)}) collective-permute-start(bf16[2,2,256,128]{3,2,1,0:T(8,128)(2,1)S(1)} %get-tuple-element.46.refs_8_), channel_id=1, source_target_pairs={{0,4},{1,5},{2,6},{3,7},{4,8},{5,9},{6,10},{7,11},{8,12},{9,13},{1... | collective-permute-start | bytes 786440 | tf_op jit(solution)/shard_map/ppermute | solution.py:22
  22.2 2.5 %collective-permute-start.7 = (bf16[2,2,256,128]{3,2,1,0:T(8,128)(2,1)S(1)}, bf16[2,2,256,128]{3,2,1,0:T(8,128)(2,1)S(1)}, u32[]{:S(2)}, u32[]{:S(2)}) collective-permute-start(bf16[2,2,256,128]{3,2,1,0:T(8,128)(2,1)S(1)} %get-tuple-element.46.refs_8_), channel_id=1, source_target_pairs={{0,2},{1,3},{2,4},{3,5},{4,6},{5,7},{6,8},{7,9},{8,10},{9,11},{10,... | collective-permute-start | bytes 786440 | tf_op jit(solution)/shard_map/ppermute | solution.py:22
  24.7 0.7 copy-done.3
  25.5 11.1 %attention_chunk.2 = (bf16[128,8,8,128]{3,2,1,0:T(8,128)(2,1)}, bf16[128,2,8,128]{3,2,1,0:T(8,128)(2,1)S(1)}, f32[2,2,256,128]{3,2,1,0:T(8,128)S(1)}, bf16[2,2,2...) custom-call(s32[1]{0:T(128)} %bitcast.scal.refs_0_, bf16[128,8,8,128]{3,2,1,0:T(8,128)(2,1)S(1)} %bitcast.12, ...), custom_call_target="tpu_custom_call" | custom-call | flops 3355443200 | bytes 4980736 | tf_op jit(solution)/shard_map/attention_chunk/pallas_call | solution.py:220
  36.6 11.1 %attention_chunk.3 = (bf16[128,8,8,128]{3,2,1,0:T(8,128)(2,1)}, bf16[128,2,8,128]{3,2,1,0:T(8,128)(2,1)S(1)}, f32[2,2,256,128]{3,2,1,0:T(8,128)S(1)}, bf16[2,2,2...) custom-call(s32[1]{0:T(128)} %bitcast.scal.refs_0_, ...), custom_call_target="tpu_custom_call", output_to_operand_aliasing={{0}: (11, {})} | custom-call | flops 3355443200 | bytes 4980736 | tf_op jit(solution)/shard_map/attention_chunk/pallas_call | solution.py:220
  47.6 2.2 %collective-permute-done.9.refs_2_ = bf16[2,2,256,128]{3,2,1,0:T(8,128)(2,1)S(1)} collective-permute-done((bf16[2,2,256,128]{3,2,1,0:T(8,128)(2,1)S(1)}, bf16[2,2,256,128]{3,2,1,0:T(8,128)(2,1)S(1)}, u32[]{:S(2)}, u32[]{:S(2)}) %collective-permute-start.9) | collective-permute-done | bytes 262176 | tf_op jit(solution)/shard_map/ppermute | solution.py:22
  49.9 4.7 %collective-permute-done.10.refs_4_ = bf16[2,2,256,128]{3,2,1,0:T(8,128)(2,1)S(1)} collective-permute-done((bf16[2,2,256,128]{3,2,1,0:T(8,128)(2,1)S(1)}, bf16[2,2,256,128]{3,2,1,0:T(8,128)(2,1)S(1)}, u32[]{:S(2)}, u32[]{:S(2)}) %collective-permute-start.10) | collective-permute-done | bytes 262176 | tf_op jit(solution)/shard_map/ppermute | solution.py:22
  54.6 2.1 %collective-permute-start.15 = (bf16[128,2,8,128]{3,2,1,0:T(8,128)(2,1)S(1)}, bf16[128,2,8,128]{3,2,1,0:T(8,128)(2,1)S(1)}, u32[]{:S(2)}, u32[]{:S(2)}) collective-permute-start(bf16[128,2,8,128]{3,2,1,0:T(8,128)(2,1)S(1)} %get-tuple-element.61), channel_id=1, source_target_pairs={{0,1},{1,0},{2,3},{3,2},{4,5},{5,4},{6,7},{7,6},{8,9},{9,8},{10,11... | collective-permute-start | bytes 1572872 | tf_op jit(solution)/shard_map/ppermute | solution.py:27
  56.7 0.1 collective-permute-start.14
  56.8 11.4 %collective-permute-done.11.refs_3_ = bf16[2,2,256,128]{3,2,1,0:T(8,128)(2,1)S(1)} collective-permute-done((bf16[2,2,256,128]{3,2,1,0:T(8,128)(2,1)S(1)}, bf16[2,2,256,128]{3,2,1,0:T(8,128)(2,1)S(1)}, u32[]{:S(2)}, u32[]{:S(2)}) %collective-permute-start.11) | collective-permute-done | bytes 262176 | tf_op jit(solution)/shard_map/ppermute | solution.py:22
  68.2 3.0 %collective-permute-done.12.refs_5_ = bf16[2,2,256,128]{3,2,1,0:T(8,128)(2,1)S(1)} collective-permute-done((bf16[2,2,256,128]{3,2,1,0:T(8,128)(2,1)S(1)}, bf16[2,2,256,128]{3,2,1,0:T(8,128)(2,1)S(1)}, u32[]{:S(2)}, u32[]{:S(2)}) %collective-permute-start.12) | collective-permute-done | bytes 262176 | tf_op jit(solution)/shard_map/ppermute | solution.py:22
  71.2 0.2 final_sum.1
  71.4 3.4 %collective-permute-start.13 = (bf16[4,2,128,128]{3,2,1,0:T(8,128)(2,1)S(1)}, bf16[4,2,128,128]{3,2,1,0:T(8,128)(2,1)S(1)}, u32[]{:S(2)}, u32[]{:S(2)}) collective-permute-start(bf16[4,2,128,128]{3,2,1,0:T(8,128)(2,1)S(1)} %get-tuple-element.58), channel_id=1, source_target_pairs={{0,1},{1,0},{2,3},{3,2},{4,5},{5,4},{6,7},{7,6},{8,9},{9,8},{10,11... | collective-permute-start | bytes 786440 | tf_op jit(solution)/shard_map/ppermute | solution.py:27
  74.8 1.2 %collective-permute-done.13.got = bf16[4,2,128,128]{3,2,1,0:T(8,128)(2,1)S(1)} collective-permute-done((bf16[4,2,128,128]{3,2,1,0:T(8,128)(2,1)S(1)}, bf16[4,2,128,128]{3,2,1,0:T(8,128)(2,1)S(1)}, u32[]{:S(2)}, u32[]{:S(2)}) %collective-permute-start.13) | collective-permute-done | bytes 262176 | tf_op jit(solution)/shard_map/ppermute | solution.py:27
  75.9 1.8 %home_heads.1 = (bf16[128,8,128]{2,1,0:T(8,128)(2,1)}, bf16[128,8,128]{2,1,0:T(8,128)(2,1)}, bf16[128,8,8,128]{3,2,1,0:T(8,128)(2,1)}) custom-call(s32[1]{0:T(128)} %bitcast.scal.refs_0_, bf16[4,2,128,128]{3,2,1,0:T(8,128)(2,1)S(1)} %get-tuple-element.57.keep, ...), custom_call_target="tpu_custom_call", output_to_operand_aliasing={{2}: (3, {})} | custom-call | bytes 3145728 | tf_op jit(solution)/shard_map/home_heads/pallas_call | solution.py:118
  (26 shorter events, 0.1 us)
Async XLA Ops:
  0.6 4.7 %collective-permute-start = (bf16[128,8,128]{2,1,0:T(8,128)(2,1)}, bf16[128,8,128]{2,1,0:T(8,128)(2,1)S(1)}, u32[]{:S(2)}, u32[]{:S(2)}) collective-permute-start(bf16[128,8,128]{2,1,0:T(8,128)(2,1)} %k.1), channel_id=1, source_target_pairs={{0,1},{1,0},{2,3},{3,2},{4,5},{5,4},{6,7},{7,6},{8,9},{9,8},{10,11... | collective-permute-start | bytes 786440 | tf_op jit(solution)/shard_map/ppermute | solution.py:27
  1.4 4.0 %collective-permute-start.1 = (bf16[128,8,128]{2,1,0:T(8,128)(2,1)}, bf16[128,8,128]{2,1,0:T(8,128)(2,1)S(1)}, u32[]{:S(2)}, u32[]{:S(2)}) collective-permute-start(bf16[128,8,128]{2,1,0:T(8,128)(2,1)} %v.1), channel_id=1, source_target_pairs={{0,1},{1,0},{2,3},{3,2},{4,5},{5,4},{6,7},{7,6},{8,9},{9,8},{10,11... | collective-permute-start | bytes 786440 | tf_op jit(solution)/shard_map/ppermute | solution.py:27
  3.2 1.0 %copy-start.1 = (bf16[128,8,128]{2,1,0:T(8,128)(2,1)S(1)}, bf16[128,8,128]{2,1,0:T(8,128)(2,1)}, u32[]{:S(2)}) copy-start(bf16[128,8,128]{2,1,0:T(8,128)(2,1)} %k.1) | copy-start | bytes 786436
  4.2 0.9 %copy-start.2 = (bf16[128,8,128]{2,1,0:T(8,128)(2,1)S(1)}, bf16[128,8,128]{2,1,0:T(8,128)(2,1)}, u32[]{:S(2)}) copy-start(bf16[128,8,128]{2,1,0:T(8,128)(2,1)} %v.1) | copy-start | bytes 786436
  5.6 19.1 %collective-permute-start.2 = (bf16[128,8,8,128]{3,2,1,0:T(8,128)(2,1)}, bf16[128,8,8,128]{3,2,1,0:T(8,128)(2,1)S(1)}, u32[]{:S(2)}, u32[]{:S(2)}) collective-permute-start(bf16[128,8,8,128]{3,2,1,0:T(8,128)(2,1)} %bitcast.11), channel_id=1, source_target_pairs={{0,1},{1,0},{2,3},{3,2},{4,5},{5,4},{6,7},{7,6},{8,9},{9,8},{10,11... | collective-permute-start | bytes 6291464 | tf_op jit(solution)/shard_map/ppermute | solution.py:27
  6.1 18.6 %collective-permute-start.3 = (bf16[128,8,8,128]{3,2,1,0:T(8,128)(2,1)}, bf16[128,8,8,128]{3,2,1,0:T(8,128)(2,1)}, u32[]{:S(2)}, u32[]{:S(2)}) collective-permute-start(bf16[128,8,8,128]{3,2,1,0:T(8,128)(2,1)} %bitcast.7), channel_id=1, source_target_pairs={{0,1},{1,0},{2,3},{3,2},{4,5},{5,4},{6,7},{7,6},{8,9},{9,8},{10,11... | collective-permute-start | bytes 6291464 | tf_op jit(solution)/shard_map/ppermute | solution.py:27
  6.2 16.0 %collective-permute-start.6 = (bf16[2,2,256,128]{3,2,1,0:T(8,128)(2,1)S(1)}, bf16[2,2,256,128]{3,2,1,0:T(8,128)(2,1)S(1)}, u32[]{:S(2)}, u32[]{:S(2)}) collective-permute-start(bf16[2,2,256,128]{3,2,1,0:T(8,128)(2,1)S(1)} %get-tuple-element.44.kv_own), channel_id=1, source_target_pairs={{0,4},{1,5},{2,6},{3,7},{4,8},{5,9},{6,10},{7,11},{8,12},{9,13},{1... | collective-permute-start | bytes 786440 | tf_op jit(solution)/shard_map/ppermute | solution.py:22
  9.6 15.1 %collective-permute-start.5 = (bf16[2,2,256,128]{3,2,1,0:T(8,128)(2,1)S(1)}, bf16[2,2,256,128]{3,2,1,0:T(8,128)(2,1)}, u32[]{:S(2)}, u32[]{:S(2)}) collective-permute-start(bf16[2,2,256,128]{3,2,1,0:T(8,128)(2,1)S(1)} %get-tuple-element.44.kv_own), channel_id=1, source_target_pairs={{0,2},{1,3},{2,4},{3,5},{4,6},{5,7},{6,8},{7,9},{8,10},{9,11},{10,... | collective-permute-start | bytes 786440 | tf_op jit(solution)/shard_map/ppermute | solution.py:22
  11.5 13.2 %copy-start = (bf16[128,64,128]{2,1,0:T(8,128)(2,1)S(1)}, bf16[128,64,128]{2,1,0:T(8,128)(2,1)}, u32[]{:S(2)}) copy-start(bf16[128,64,128]{2,1,0:T(8,128)(2,1)} %param.11) | copy-start | bytes 6291460
  11.5 13.2 %copy-start.5 = (bf16[128,64,128]{2,1,0:T(8,128)(2,1)S(1)}, bf16[128,64,128]{2,1,0:T(8,128)(2,1)}, u32[]{:S(2)}) copy-start(bf16[128,64,128]{2,1,0:T(8,128)(2,1)} %param.7) | copy-start | bytes 6291460
  18.2 2.0 %collective-permute-start.4 = (f32[8,1,1024]{2,1,0:T(1,128)}, f32[8,1,1024]{2,1,0:T(1,128)S(1)}, u32[]{:S(2)}, u32[]{:S(2)}) collective-permute-start(f32[8,1,1024]{2,1,0:T(1,128)} %delta.1.d_own.refs_5_), channel_id=1, source_target_pairs={{0,1},{1,0},{2,3},{3,2},{4,5},{5,4},{6,7},{7,6},{8,9},{9,8},{10,11... | collective-permute-start | bytes 98312 | tf_op jit(solution)/shard_map/ppermute | solution.py:27
  20.2 16.3 %collective-permute-start.8 = (bf16[2,2,256,128]{3,2,1,0:T(8,128)(2,1)S(1)}, bf16[2,2,256,128]{3,2,1,0:T(8,128)(2,1)S(1)}, u32[]{:S(2)}, u32[]{:S(2)}) collective-permute-start(bf16[2,2,256,128]{3,2,1,0:T(8,128)(2,1)S(1)} %get-tuple-element.46.refs_8_), channel_id=1, source_target_pairs={{0,4},{1,5},{2,6},{3,7},{4,8},{5,9},{6,10},{7,11},{8,12},{9,13},{1... | collective-permute-start | bytes 786440 | tf_op jit(solution)/shard_map/ppermute | solution.py:22
  22.2 14.4 %collective-permute-start.7 = (bf16[2,2,256,128]{3,2,1,0:T(8,128)(2,1)S(1)}, bf16[2,2,256,128]{3,2,1,0:T(8,128)(2,1)S(1)}, u32[]{:S(2)}, u32[]{:S(2)}) collective-permute-start(bf16[2,2,256,128]{3,2,1,0:T(8,128)(2,1)S(1)} %get-tuple-element.46.refs_8_), channel_id=1, source_target_pairs={{0,2},{1,3},{2,4},{3,5},{4,6},{5,7},{6,8},{7,9},{8,10},{9,11},{10,... | collective-permute-start | bytes 786440 | tf_op jit(solution)/shard_map/ppermute | solution.py:22
  24.7 0.8 copy-start.3
  25.5 11.1 %copy-start.4 = (f32[8,1,1024]{2,1,0:T(1,128)S(1)}, f32[8,1,1024]{2,1,0:T(1,128)}, u32[]{:S(2)}) copy-start(f32[8,1,1024]{2,1,0:T(1,128)} %delta.1.d_own.refs_5_) | copy-start | bytes 98308
  36.5 13.3 %collective-permute-start.9 = (bf16[2,2,256,128]{3,2,1,0:T(8,128)(2,1)S(1)}, bf16[2,2,256,128]{3,2,1,0:T(8,128)(2,1)S(1)}, u32[]{:S(2)}, u32[]{:S(2)}) collective-permute-start(bf16[2,2,256,128]{3,2,1,0:T(8,128)(2,1)S(1)} %get-tuple-element.51), channel_id=1, source_target_pairs={{0,252},{1,253},{2,254},{3,255},{4,0},{5,1},{6,2},{7,3},{8,4},{9,5... | collective-permute-start | bytes 786440 | tf_op jit(solution)/shard_map/ppermute | solution.py:22
  36.5 18.1 %collective-permute-start.10 = (bf16[2,2,256,128]{3,2,1,0:T(8,128)(2,1)S(1)}, bf16[2,2,256,128]{3,2,1,0:T(8,128)(2,1)S(1)}, u32[]{:S(2)}, u32[]{:S(2)}) collective-permute-start(bf16[2,2,256,128]{3,2,1,0:T(8,128)(2,1)S(1)} %get-tuple-element.52), channel_id=1, source_target_pairs={{0,254},{1,255},{2,0},{3,1},{4,2},{5,3},{6,4},{7,5},{8,6},{9,7},{1... | collective-permute-start | bytes 786440 | tf_op jit(solution)/shard_map/ppermute | solution.py:22
  54.6 13.6 %collective-permute-start.11 = (bf16[2,2,256,128]{3,2,1,0:T(8,128)(2,1)S(1)}, bf16[2,2,256,128]{3,2,1,0:T(8,128)(2,1)S(1)}, u32[]{:S(2)}, u32[]{:S(2)}) collective-permute-start(bf16[2,2,256,128]{3,2,1,0:T(8,128)(2,1)S(1)} %get-tuple-element.54), channel_id=1, source_target_pairs={{0,252},{1,253},{2,254},{3,255},{4,0},{5,1},{6,2},{7,3},{8,4},{9,5... | collective-permute-start | bytes 786440 | tf_op jit(solution)/shard_map/ppermute | solution.py:22
  54.6 16.7 %collective-permute-start.12 = (bf16[2,2,256,128]{3,2,1,0:T(8,128)(2,1)S(1)}, bf16[2,2,256,128]{3,2,1,0:T(8,128)(2,1)S(1)}, u32[]{:S(2)}, u32[]{:S(2)}) collective-permute-start(bf16[2,2,256,128]{3,2,1,0:T(8,128)(2,1)S(1)} %get-tuple-element.56), channel_id=1, source_target_pairs={{0,254},{1,255},{2,0},{3,1},{4,2},{5,3},{6,4},{7,5},{8,6},{9,7},{1... | collective-permute-start | bytes 786440 | tf_op jit(solution)/shard_map/ppermute | solution.py:22
  54.6 20.2 %collective-permute-start.15 = (bf16[128,2,8,128]{3,2,1,0:T(8,128)(2,1)S(1)}, bf16[128,2,8,128]{3,2,1,0:T(8,128)(2,1)S(1)}, u32[]{:S(2)}, u32[]{:S(2)}) collective-permute-start(bf16[128,2,8,128]{3,2,1,0:T(8,128)(2,1)S(1)} %get-tuple-element.61), channel_id=1, source_target_pairs={{0,1},{1,0},{2,3},{3,2},{4,5},{5,4},{6,7},{7,6},{8,9},{9,8},{10,11... | collective-permute-start | bytes 1572872 | tf_op jit(solution)/shard_map/ppermute | solution.py:27
  56.7 18.1 %collective-permute-start.14 = (bf16[128,2,8,128]{3,2,1,0:T(8,128)(2,1)S(1)}, bf16[128,2,8,128]{3,2,1,0:T(8,128)(2,1)S(1)}, u32[]{:S(2)}, u32[]{:S(2)}) collective-permute-start(bf16[128,2,8,128]{3,2,1,0:T(8,128)(2,1)S(1)} %get-tuple-element.60), channel_id=1, source_target_pairs={{0,1},{1,0},{2,3},{3,2},{4,5},{5,4},{6,7},{7,6},{8,9},{9,8},{10,11... | collective-permute-start | bytes 1572872 | tf_op jit(solution)/shard_map/ppermute | solution.py:27
  71.4 4.5 %collective-permute-start.13 = (bf16[4,2,128,128]{3,2,1,0:T(8,128)(2,1)S(1)}, bf16[4,2,128,128]{3,2,1,0:T(8,128)(2,1)S(1)}, u32[]{:S(2)}, u32[]{:S(2)}) collective-permute-start(bf16[4,2,128,128]{3,2,1,0:T(8,128)(2,1)S(1)} %get-tuple-element.58), channel_id=1, source_target_pairs={{0,1},{1,0},{2,3},{3,2},{4,5},{5,4},{6,7},{7,6},{8,9},{9,8},{10,11... | collective-permute-start | bytes 786440 | tf_op jit(solution)/shard_map/ppermute | solution.py:27
